TPU v7x, 32 devices: a whole 2x2x4 slice. The times are simulated.
32 devices in a mesh: groups: 2 (over y), blocks: 4 (over z), tiles: 2 (over x), sub: 2 (over core).
Axes of the slice: x: 2, y: 2, z: 4, core: 2. Of those that a mesh axis runs over, the one named last changes fastest.
Arguments:
- seg_feat: bfloat16 [8, 4, 2048, 128], P(('groups', 'tiles', 'sub'), 'blocks'), parts along dimension 0, may hold values from -6 to 6
- seg_block: int32 [8, 4, 2048, 1], P(('groups', 'tiles', 'sub'), 'blocks'), parts along dimension 0, may hold values from 0 to 3; in each aligned block of 2048 rows (0 to 2047, 2048 to 4095, ..., all dimensions but the last counted through in order) at most 1024 rows name the same one
- depth_rank: int32 [8, 4, 8, 256], P(('groups', 'tiles', 'sub'), 'blocks'), parts along dimension 0, may hold values from 0 to 7, as said below
- w_in: bfloat16 [4, 128, 512], P('blocks'), may hold values from -0.5 to 0.5
- w_hidden: bfloat16 [4, 4, 512, 512], P('blocks'), may hold values from -0.25 to 0.25
- w_out: bfloat16 [4, 512, 128], P('blocks'), may hold values from -0.25 to 0.25
- w_dens: bfloat16 [4, 512], P('blocks'), may hold values from -0.25 to 0.25
- conv_w: bfloat16 [3, 3, 3, 128, 128], replicated, may hold values from -0.1875 to 0.1875
Outputs:
- decoded: bfloat16 [128, 64, 128], P(('groups', 'tiles', 'sub'), 'blocks'), parts along dimension 0
There are 2 independent parts, one for each index of `groups`. A program takes and returns all parts, laid end to end along the dimension named above; an argument that names none is the same for every part. Nothing has to cross between parts.
Inputs may be any that keep to these rules, and one draw needn't show every extreme that they name: `seg_block`: among one device's 2048 segments, no block is named more than 1024 times; some device names some block exactly 1024 times. `depth_rank`: for every ray, its 8 segments' ranks are a permutation of 0 .. 7.
All inputs are finite; a program needn't handle non-finite values.
Results may differ from a plain program's by a relative error of at most 0.02.
Values may be sent and summed in bfloat16 or wider, within the bound.
No kernel may reach another device: no remote copies, remote signals or barrier semaphores. Data moves between devices by JAX's collectives and lax.ppermute only.
A program may use at most 64 MiB of HBM per device.

v0:
```python
import jax
import jax.numpy as jnp
from jax import lax
from jax.sharding import PartitionSpec as P

SEGS_RAY = 8
CONV_LAYERS = 3
TW = 16
TH = 16
RAYS_DEV = 256


def with_halo(shard, sides, width):
    for axis, dim in sides:
        peers, length = (lax.axis_size(axis), shard.shape[dim])
        up = [(i, (i + 1) % peers) for i in range(peers - 1)]
        down = [(j, i) for i, j in up]
        last = lax.slice_in_dim(shard, length - width, length, axis=dim)
        initial = lax.slice_in_dim(shard, 0, width, axis=dim)
        before = lax.ppermute(last, axis, up)
        after = lax.ppermute(initial, axis, down)
        shard = jnp.concatenate([before, shard, after], axis=dim)
    return shard


def place_rows(block_ids, capacity, block_count):
    onehot = (block_ids[:, None] == jnp.arange(block_count, dtype=jnp.int32)[None, :]).astype(
        jnp.int32
    )
    before = jnp.cumsum(onehot, axis=0) - onehot
    return block_ids * capacity + jnp.sum(before * onehot, axis=1)


def evaluate(row_block, first_weight, hidden, last_weight, density_row):
    hidden_act = jax.nn.silu(
        jnp.dot(row_block, first_weight, preferred_element_type=jnp.float32)
    ).astype(jnp.bfloat16)
    for layer_index in range(hidden.shape[0]):
        update = jax.nn.silu(
            jnp.dot(hidden_act, hidden[layer_index], preferred_element_type=jnp.float32)
        )
        hidden_act = (hidden_act.astype(jnp.float32) + update).astype(jnp.bfloat16)
    features = jnp.dot(hidden_act, last_weight, preferred_element_type=jnp.float32).astype(
        jnp.bfloat16
    )
    raw_density = jnp.dot(hidden_act, density_row, preferred_element_type=jnp.float32)
    density = (0.25 * jax.nn.softplus(raw_density)).astype(jnp.bfloat16)
    return (features, density)


def composite(features, density, rank_table):
    density_f32 = density.astype(jnp.float32)
    in_front = (rank_table[:, None, :] < rank_table[None, :, :]).astype(jnp.float32)
    optical = jnp.sum(density_f32[:, None, :] * in_front, axis=0)
    weight = jnp.exp(-optical) * (1.0 - jnp.exp(-density_f32))
    pixel_color = jnp.sum(weight[:, :, None] * features.astype(jnp.float32), axis=0)
    return pixel_color.astype(jnp.bfloat16)


def conv_layer(padded, kernel, out_rows, out_cols):
    pieces = []
    for offset_y in range(3):
        for offset_x in range(3):
            pieces.append(padded[offset_y : offset_y + out_rows, offset_x : offset_x + out_cols])
    patches = jnp.concatenate(pieces, axis=-1)
    channels = kernel.shape[-1]
    result = jnp.dot(
        patches, kernel.reshape(9 * kernel.shape[2], channels), preferred_element_type=jnp.float32
    )
    center = padded[1 : 1 + out_rows, 1 : 1 + out_cols].astype(jnp.float32)
    return (center + jax.nn.silu(result)).astype(jnp.bfloat16)


def shards(seg_feat, seg_block, depth_rank, w_in, w_hidden, w_out, w_dens, conv_w):
    local_rows = seg_feat[0, 0]
    block_ids = seg_block[0, 0, :, 0]
    rank_table = depth_rank[0, 0]
    block_count = lax.axis_size("blocks")
    segments = local_rows.shape[0]
    in_width = local_rows.shape[1]
    capacity = 2 * segments // block_count
    slot_index = place_rows(block_ids, capacity, block_count)
    sendbuf = (
        jnp.zeros((block_count * capacity, in_width), jnp.bfloat16).at[slot_index].set(local_rows)
    )
    sendbuf = sendbuf.reshape(block_count, capacity, in_width)
    first_weight = w_in[0]
    hidden = w_hidden[0]
    last_weight = w_out[0]
    density_row = w_dens[0]
    out_width = last_weight.shape[1]
    received = lax.all_to_all(sendbuf, "blocks", split_axis=0, concat_axis=0, tiled=True)
    sources = received.shape[0]
    count_items = received.shape[1]
    features, density = evaluate(
        received.reshape(sources * count_items, in_width),
        first_weight,
        hidden,
        last_weight,
        density_row,
    )
    features, density = (
        features.reshape(sources, count_items, out_width),
        density.reshape(sources, count_items),
    )
    feat_back, density_back = (
        lax.all_to_all(features, "blocks", split_axis=0, concat_axis=0, tiled=True),
        lax.all_to_all(density, "blocks", split_axis=0, concat_axis=0, tiled=True),
    )
    feat_seg = feat_back.reshape(block_count * capacity, out_width)[slot_index].reshape(
        SEGS_RAY, RAYS_DEV, out_width
    )
    density_seg = density_back.reshape(block_count * capacity)[slot_index].reshape(
        SEGS_RAY, RAYS_DEV
    )
    tile_image = composite(feat_seg, density_seg, rank_table).reshape(TH, TW, out_width)
    rows_total = TH * lax.axis_size(("tiles", "sub"))
    cols_total = TW * block_count
    row_pos = (
        lax.axis_index(("tiles", "sub")) * TH
        - CONV_LAYERS
        + jnp.arange(TH + 2 * CONV_LAYERS, dtype=jnp.int32)
    )
    col_pos = (
        lax.axis_index("blocks") * TW
        - CONV_LAYERS
        + jnp.arange(TW + 2 * CONV_LAYERS, dtype=jnp.int32)
    )
    inside = ((row_pos >= 0) & (row_pos < rows_total))[:, None] & (
        (col_pos >= 0) & (col_pos < cols_total)
    )[None, :]
    current = with_halo(tile_image, (("blocks", 1), (("tiles", "sub"), 0)), CONV_LAYERS)
    for layer_index in range(CONV_LAYERS):
        margin = CONV_LAYERS - layer_index - 1
        size_h = TH + 2 * margin
        size_w = TW + 2 * margin
        current = conv_layer(current, conv_w[layer_index], size_h, size_w)
        keep_mask = inside[
            layer_index + 1 : layer_index + 1 + size_h, layer_index + 1 : layer_index + 1 + size_w
        ]
        current = jnp.where(keep_mask[:, :, None], current, jnp.zeros_like(current))
    tile_image = current
    return tile_image


def solution(mesh):
    in_specs = (
        P(("groups", "tiles", "sub"), "blocks", None, None),
        P(("groups", "tiles", "sub"), "blocks", None, None),
        P(("groups", "tiles", "sub"), "blocks", None, None),
        P("blocks", None, None),
        P("blocks", None, None, None),
        P("blocks", None, None),
        P("blocks", None),
        P(),
    )
    out_specs = P(("groups", "tiles", "sub"), "blocks", None)
    return jax.shard_map(shards, mesh=mesh, in_specs=in_specs, out_specs=out_specs, check_vma=False)
```

profile of v0, /device:TPU:1, one launch (start us, length us, event | category | flops | bytes accessed | tf_op | source)
XLA Modules:
  0.0 131.0 jit_solution(11247792190013034700)
XLA Ops:
  0.0 0.0 copy-start
  0.0 0.8 fusion.27
  0.8 1.1 reduce-window.6
  1.9 0.2 slice_reduce_fusion
  2.1 0.2 reduce-window.9
  2.3 0.1 add_bitcast_fusion
  2.4 0.7 fusion.26
  3.1 0.7 compare_select_fusion
  3.8 0.0 copy-done
  3.9 6.1 %scatter_custom_fusion = bf16[4096,128]{1,0:T(8,128)(2,1)S(1)} fusion(s32[2048]{0:T(1024)S(1)} %bitcast.102, bf16[1,1,2048,128]{3,2,1,0:T(8,128)(2,1)S(1)} %copy-done, bf16[]{:T(256)} %constant.53.clone.1), kind=kCustom, calls=%fused_computation.19 | custom fusion | bytes 1572866 | tf_op jit(solution)/shard_map/scatter | solution.py:84
  9.9 30.1 %all_to_all.20 = bf16[4,1024,128]{2,1,0:T(8,128)(2,1)S(1)} all-to-all(bf16[4,1024,128]{2,1,0:T(8,128)(2,1)S(1)} %bitcast.90), channel_id=1, replica_groups=mesh['groups'=2,'blocks'=4,'tiles'=2,'sub'=2] {'blocks'}, dimensions={0} | all-to-all | bytes 2097152 | tf_op jit(solution)/shard_map/all_to_all | solution.py:92
  40.1 3.6 %multiply_convert_fusion = bf16[4096,512]{1,0:T(8,128)(2,1)S(1)} fusion(bf16[4096,128]{1,0:T(8,128)(2,1)S(1)} %bitcast.92, bf16[1,128,512]{2,1,0:T(8,128)(2,1)} %param.11), kind=kOutput, calls=%fused_computation.7 | convolution fusion | flops 547356672 | bytes 5373952 | tf_op jit(solution)/shard_map/dot_general | solution.py:36
  43.7 0.0 copy-done.3
  43.7 2.3 %fusion.11 = f32[4096,512]{1,0:T(8,128)S(1)} fusion(bf16[4096,512]{1,0:T(8,128)(2,1)S(1)} %multiply_convert_fusion, bf16[1,4,512,512]{3,2,1,0:T(8,128)(2,1)S(1)} %copy-done.3), kind=kOutput, calls=%fused_computation.17 | convolution fusion | flops 2147483648 | bytes 13107200 | tf_op jit(solution)/shard_map/dot_general | solution.py:40
  46.0 6.9 %add_convert_fusion.2 = bf16[4096,512]{1,0:T(8,128)(2,1)S(1)} fusion(f32[4096,512]{1,0:T(8,128)S(1)} %fusion.11, bf16[4096,512]{1,0:T(8,128)(2,1)S(1)} %multiply_convert_fusion, bf16[1,4,512,512]{3,2,1,0:T(8,128)(2,1)S(1)} %copy-done.3), kind=kOutput, calls=%fused_computation.5 | convolution fusion | flops 2191523840 | bytes 29884416 | tf_op jit(solution)/shard_map/dot_general | solution.py:40
  52.9 2.3 %fusion.5 = f32[4096,512]{1,0:T(8,128)S(1)} fusion(bf16[4096,512]{1,0:T(8,128)(2,1)S(1)} %add_convert_fusion.2, bf16[1,4,512,512]{3,2,1,0:T(8,128)(2,1)S(1)} %copy-done.3), kind=kOutput, calls=%fused_computation.13 | convolution fusion | flops 2147483648 | bytes 13107200 | tf_op jit(solution)/shard_map/dot_general | solution.py:40
  55.2 0.0 copy-start.6
  55.3 6.9 %add_convert_fusion = bf16[4096,512]{1,0:T(8,128)(2,1)S(1)} fusion(f32[4096,512]{1,0:T(8,128)S(1)} %fusion.5, bf16[4096,512]{1,0:T(8,128)(2,1)S(1)} %add_convert_fusion.2, bf16[1,4,512,512]{3,2,1,0:T(8,128)(2,1)S(1)} %copy-done.3), kind=kOutput, calls=%fused_computation.3 | convolution fusion | flops 2191523840 | bytes 29884416 | tf_op jit(solution)/shard_map/dot_general | solution.py:40
  62.1 0.0 copy-start.1
  62.1 1.9 %copy-done.1 = bf16[4096,512]{1,0:T(8,128)(2,1)} copy-done((bf16[4096,512]{1,0:T(8,128)(2,1)}, bf16[4096,512]{1,0:T(8,128)(2,1)S(1)}, u32[]{:S(2)}) %copy-start.1) | copy-done | bytes 4194328
  64.1 0.0 copy-done.6
  64.1 1.2 fusion.30
  65.3 0.5 broadcast.119
  65.8 0.7 reduce.3
  66.5 0.6 reshape.161
  67.1 3.4 %all-to-all-start.1 = ((bf16[4,2,512]{2,1,0:T(2,128)(2,1)}), bf16[4,2,512]{2,1,0:T(2,128)(2,1)S(1)}, u32[]{:S(2)}, u32[]{:S(2)}) async-start(bf16[4,2,512]{2,1,0:T(2,128)(2,1)} %reshape.161), calls=%async_computation.1 | async-start | bytes 16384 | tf_op jit(solution)/shard_map/all_to_all | solution.py:108
  70.6 0.0 copy-done.4
  70.6 0.0 copy-start.2
  70.6 4.5 %convolution_convert_fusion = bf16[4096,128]{1,0:T(8,128)(2,1)} fusion(bf16[4096,512]{1,0:T(8,128)(2,1)} %copy-done.1, bf16[1,512,128]{2,1,0:T(8,128)(2,1)S(1)} %copy-done.4), kind=kOutput, calls=%fused_computation.8 | convolution fusion | flops 537395200 | bytes 5373952 | tf_op jit(solution)/shard_map/dot_general | solution.py:43
  75.1 0.0 all-to-all-done.1
  75.1 4.4 %all-to-all-start.2 = ((bf16[4,1024,128]{2,1,0:T(8,128)(2,1)}), bf16[4,1024,128]{2,1,0:T(8,128)(2,1)S(1)}, u32[]{:S(2)}, u32[]{:S(2)}) async-start(bf16[4,1024,128]{2,1,0:T(8,128)(2,1)} %bitcast.17), calls=%async_computation.2 | async-start | bytes 2097152 | tf_op jit(solution)/shard_map/all_to_all | solution.py:107
  79.5 0.0 copy-done.2
  79.5 0.1 fusion.34
  79.7 0.1 reduce.1
  79.7 13.1 %gather_fusion = bf16[2048]{0:T(1024)(128)(2,1)S(1)} fusion(bf16[4096]{0:T(1024)(128)(2,1)S(1)} %bitcast.88, s32[2048]{0:T(1024)S(1)} %broadcast_clamp_fusion), kind=kCustom, calls=%fused_computation | custom fusion | bytes 16384 | tf_op jit(solution)/shard_map/gather | solution.py:113
  92.9 11.9 %all-to-all-done.2 = bf16[4,1024,128]{2,1,0:T(8,128)(2,1)S(1)} async-done(((bf16[4,1024,128]{2,1,0:T(8,128)(2,1)}), bf16[4,1024,128]{2,1,0:T(8,128)(2,1)S(1)}, u32[]{:S(2)}, u32[]{:S(2)}) %all-to-all-start.2) | async-done | bytes 1048608 | tf_op jit(solution)/shard_map/all_to_all | solution.py:107
  104.8 6.2 %gather_fusion.1 = bf16[2048,128]{1,0:T(8,128)(2,1)S(1)} fusion(bf16[4096,128]{1,0:T(8,128)(2,1)S(1)} %bitcast.89, s32[2048]{0:T(1024)S(1)} %broadcast_clamp_fusion), kind=kCustom, calls=%fused_computation.1 | custom fusion | bytes 1056768 | tf_op jit(solution)/shard_map/gather | solution.py:110
  111.0 0.3 fusion
  111.4 1.3 collective-permute-start
  112.7 1.3 collective-permute-start.1
  114.0 0.0 collective-permute-done
  114.0 3.2 %collective-permute-done.1 = bf16[16,3,128]{2,1,0:T(4,128)(2,1)S(1)} collective-permute-done((bf16[16,3,128]{2,1,0:T(4,128)(2,1)S(1)}, bf16[16,3,128]{2,1,0:T(4,128)(2,1)S(1)}, u32[]{:S(2)}, u32[]{:S(2)}) %collective-permute-start.1) | collective-permute-done | bytes 12320 | tf_op jit(solution)/shard_map/ppermute | solution.py:21
  117.2 5.5 %collective-permute-start.2 = (bf16[3,22,128]{2,1,0:T(8,128)(2,1)S(1)}, bf16[3,22,128]{2,1,0:T(8,128)(2,1)S(1)}, u32[]{:S(2)}, u32[]{:S(2)}) collective-permute-start(bf16[3,22,128]{2,1,0:T(8,128)(2,1)S(1)} %get-tuple-element.8), channel_id=1, source_target_pairs={{0,1},{1,2},{2,3},{4,5},{5,6},{6,7},{8,9},{9,10},{10,11},{12,13},{... | collective-permute-start | bytes 50696 | tf_op jit(solution)/shard_map/ppermute | solution.py:20
  122.7 1.9 %collective-permute-start.3 = (bf16[3,22,128]{2,1,0:T(8,128)(2,1)S(1)}, bf16[3,22,128]{2,1,0:T(8,128)(2,1)S(1)}, u32[]{:S(2)}, u32[]{:S(2)}) collective-permute-start(bf16[3,22,128]{2,1,0:T(8,128)(2,1)S(1)} %get-tuple-element.9), channel_id=1, source_target_pairs={{1,0},{2,1},{3,2},{5,4},{6,5},{7,6},{9,8},{10,9},{11,10},{13,12},{... | collective-permute-start | bytes 50696 | tf_op jit(solution)/shard_map/ppermute | solution.py:21
  124.6 0.1 broadcast_and_fusion
  124.7 0.1 slice.185
  124.8 0.1 slice.184
  124.9 0.1 slice.183
  124.9 0.0 collective-permute-done.2
  124.9 2.8 %collective-permute-done.3 = bf16[3,22,128]{2,1,0:T(8,128)(2,1)S(1)} collective-permute-done((bf16[3,22,128]{2,1,0:T(8,128)(2,1)S(1)}, bf16[3,22,128]{2,1,0:T(8,128)(2,1)S(1)}, u32[]{:S(2)}, u32[]{:S(2)}) %collective-permute-start.3) | collective-permute-done | bytes 16928 | tf_op jit(solution)/shard_map/ppermute | solution.py:21
  127.8 0.1 pad_maximum_fusion
  127.9 0.1 slice_dynamic-update-slice_fusion.6
  127.9 0.1 slice_dynamic-update-slice_fusion.5
  128.0 0.1 slice_dynamic-update-slice_fusion.16
  128.1 0.1 slice_dynamic-update-slice_fusion.3
  128.2 0.1 slice_dynamic-update-slice_fusion.1
  128.3 0.1 slice_dynamic-update-slice_fusion
  128.3 0.5 broadcast_select_fusion
  128.9 0.1 slice_dynamic-update-slice_fusion.14
  128.9 0.1 slice_dynamic-update-slice_fusion.13
  129.0 0.1 slice_dynamic-update-slice_fusion.17
  129.1 0.1 slice_dynamic-update-slice_fusion.11
  129.3 0.5 fusion.20
  130.1 1.0 fusion.23
  (32 shorter events, 0.7 us)
Async XLA Ops:
  0.0 3.9 %copy-start = (bf16[1,1,2048,128]{3,2,1,0:T(8,128)(2,1)S(1)}, bf16[1,1,2048,128]{3,2,1,0:T(8,128)(2,1)}, u32[]{:S(2)}) copy-start(bf16[1,1,2048,128]{3,2,1,0:T(8,128)(2,1)} %param.8) | copy-start | bytes 1572868
  40.1 3.6 %copy-start.3 = (bf16[1,4,512,512]{3,2,1,0:T(8,128)(2,1)S(1)}, bf16[1,4,512,512]{3,2,1,0:T(8,128)(2,1)}, u32[]{:S(2)}) copy-start(bf16[1,4,512,512]{3,2,1,0:T(8,128)(2,1)} %param.12) | copy-start | bytes 6291460
  55.2 8.8 %copy-start.6 = (bf16[1,512]{1,0:T(2,128)(2,1)S(1)}, bf16[1,512]{1,0:T(2,128)(2,1)}, u32[]{:S(2)}) copy-start(bf16[1,512]{1,0:T(2,128)(2,1)} %param.14) | copy-start | bytes 3076
  62.1 1.9 %copy-start.1 = (bf16[4096,512]{1,0:T(8,128)(2,1)}, bf16[4096,512]{1,0:T(8,128)(2,1)S(1)}, u32[]{:S(2)}) copy-start(bf16[4096,512]{1,0:T(8,128)(2,1)S(1)} %add_convert_fusion) | copy-start | bytes 12582916
  64.1 6.5 %copy-start.4 = (bf16[1,512,128]{2,1,0:T(8,128)(2,1)S(1)}, bf16[1,512,128]{2,1,0:T(8,128)(2,1)}, u32[]{:S(2)}) copy-start(bf16[1,512,128]{2,1,0:T(8,128)(2,1)} %param.13) | copy-start | bytes 393220
  67.1 8.0 %all-to-all-start.1 = ((bf16[4,2,512]{2,1,0:T(2,128)(2,1)}), bf16[4,2,512]{2,1,0:T(2,128)(2,1)S(1)}, u32[]{:S(2)}, u32[]{:S(2)}) async-start(bf16[4,2,512]{2,1,0:T(2,128)(2,1)} %reshape.161), calls=%async_computation.1 | async-start | bytes 16384 | tf_op jit(solution)/shard_map/all_to_all | solution.py:108
  70.6 9.0 %copy-start.2 = (bf16[3,3,3,128,128]{4,3,2,1,0:T(8,128)(2,1)S(1)}, bf16[3,3,3,128,128]{4,3,2,1,0:T(8,128)(2,1)}, u32[]{:S(2)}) copy-start(bf16[3,3,3,128,128]{4,3,2,1,0:T(8,128)(2,1)} %param.15) | copy-start | bytes 2654212
  75.1 17.7 %copy-start.5 = (s32[1,1,8,256]{3,2,1,0:T(8,128)S(1)}, s32[1,1,8,256]{3,2,1,0:T(8,128)}, u32[]{:S(2)}) copy-start(s32[1,1,8,256]{3,2,1,0:T(8,128)} %param.10) | copy-start | bytes 24580
  75.1 29.7 %all-to-all-start.2 = ((bf16[4,1024,128]{2,1,0:T(8,128)(2,1)}), bf16[4,1024,128]{2,1,0:T(8,128)(2,1)S(1)}, u32[]{:S(2)}, u32[]{:S(2)}) async-start(bf16[4,1024,128]{2,1,0:T(8,128)(2,1)} %bitcast.17), calls=%async_computation.2 | async-start | bytes 2097152 | tf_op jit(solution)/shard_map/all_to_all | solution.py:107
  111.4 2.6 %collective-permute-start = (bf16[16,3,128]{2,1,0:T(4,128)(2,1)S(1)}, bf16[16,3,128]{2,1,0:T(4,128)(2,1)S(1)}, u32[]{:S(2)}, u32[]{:S(2)}) collective-permute-start(bf16[16,3,128]{2,1,0:T(4,128)(2,1)S(1)} %get-tuple-element.10), channel_id=1, source_target_pairs={{0,4},{4,8},{8,12},{1,5},{5,9},{9,13},{2,6},{6,10},{10,14},{3,7},{... | collective-permute-start | bytes 36872 | tf_op jit(solution)/shard_map/ppermute | solution.py:20
  112.7 4.5 %collective-permute-start.1 = (bf16[16,3,128]{2,1,0:T(4,128)(2,1)S(1)}, bf16[16,3,128]{2,1,0:T(4,128)(2,1)S(1)}, u32[]{:S(2)}, u32[]{:S(2)}) collective-permute-start(bf16[16,3,128]{2,1,0:T(4,128)(2,1)S(1)} %get-tuple-element.11), channel_id=1, source_target_pairs={{4,0},{8,4},{12,8},{5,1},{9,5},{13,9},{6,2},{10,6},{14,10},{7,3},{... | collective-permute-start | bytes 36872 | tf_op jit(solution)/shard_map/ppermute | solution.py:21
  117.2 7.8 %collective-permute-start.2 = (bf16[3,22,128]{2,1,0:T(8,128)(2,1)S(1)}, bf16[3,22,128]{2,1,0:T(8,128)(2,1)S(1)}, u32[]{:S(2)}, u32[]{:S(2)}) collective-permute-start(bf16[3,22,128]{2,1,0:T(8,128)(2,1)S(1)} %get-tuple-element.8), channel_id=1, source_target_pairs={{0,1},{1,2},{2,3},{4,5},{5,6},{6,7},{8,9},{9,10},{10,11},{12,13},{... | collective-permute-start | bytes 50696 | tf_op jit(solution)/shard_map/ppermute | solution.py:20
  122.7 5.1 %collective-permute-start.3 = (bf16[3,22,128]{2,1,0:T(8,128)(2,1)S(1)}, bf16[3,22,128]{2,1,0:T(8,128)(2,1)S(1)}, u32[]{:S(2)}, u32[]{:S(2)}) collective-permute-start(bf16[3,22,128]{2,1,0:T(8,128)(2,1)S(1)} %get-tuple-element.9), channel_id=1, source_target_pairs={{1,0},{2,1},{3,2},{5,4},{6,5},{7,6},{9,8},{10,9},{11,10},{13,12},{... | collective-permute-start | bytes 50696 | tf_op jit(solution)/shard_map/ppermute | solution.py:21
where the time goes:
time: 132 us; the launch traced here: 131 us
  local copies, waits for them, and re-layouts  30.1 us (23%)
  blocking collectives  30.1 us (23%)
  matrix products  29.7 us (22%)
  starting transfers between devices  17.9 us (14%)
  waiting for transfers between devices  17.9 us (14%)
  other arithmetic  4.93 us (4%)
    all_to_all x1, blocking collectives, shards(): lax.all_to_all(sendbuf, 'blocks', split_axis=0, concat_axis=0, tiled=True)  30.1 us
    dot_general x4, matrix products, evaluate(): jnp.dot(hidden_act, hidden[layer_index], preferred_element_type=jnp.float32)  18.4 us
    gather x1, local copies, waits for them, and re-layouts, shards(): density_back.reshape(block_count * capacity)[slot_index]  13.1 us
    all_to_all x1, waiting for transfers between devices, shards(): lax.all_to_all(features, 'blocks', split_axis=0, concat_axis=0, tiled=True)  11.9 us
    ppermute x2, starting transfers between devices, with_halo(): before = lax.ppermute(last, axis, up)  6.81 us
    gather x1, local copies, waits for them, and re-layouts, shards(): feat_back.reshape(block_count * capacity, out_width)[slot_index]  6.18 us
    scatter x1, local copies, waits for them, and re-layouts, shards(): jnp.zeros((block_count * capacity, in_width), jnp.bfloat16).at[slot_index]  6.05 us
    ppermute x2, waiting for transfers between devices, with_halo(): after = lax.ppermute(initial, axis, down)  6 us
  transfers between devices with their start and end apart: 6, of which 3 were waited for; matrix products, arithmetic and copies ran while one was open for 14% of the time, Pallas kernels for 0%

commit v1 on v0

v1 whole, which is shorter than its diff:
```python
import functools

import jax
import jax.numpy as jnp
from jax import lax
from jax.experimental import pallas as pl
from jax.experimental.pallas import tpu as pltpu
from jax.sharding import PartitionSpec as P

SEGS_RAY = 8
CONV_LAYERS = 3
TW = 16
TH = 16
RAYS_DEV = 256
LANES = 128
ALIGN = 16
EDGE = CONV_LAYERS * TH

F32 = jnp.float32
BF16 = jnp.bfloat16
I32 = jnp.int32


def iota(shape, dim):
    return lax.broadcasted_iota(I32, shape, dim)


def dot(a, b):
    return jnp.dot(a, b, preferred_element_type=F32)


def dot_nt(a, b):
    return lax.dot_general(a, b, (((1,), (1,)), ((), ())), preferred_element_type=F32)


def dot_tn(a, b):
    return lax.dot_general(a, b, (((0,), (0,)), ((), ())), preferred_element_type=F32)


def silu(x):
    z = 0.5 * x
    return z + z * jnp.tanh(z)


def meta_rows(capacity):
    return -(-capacity // (8 * LANES)) * 8


def pack_kernel(count, capacity, me_ref, feat_ref, block_ref, rank_ref, *rest):
    outs, packed = rest[:count], rest[count]
    me = me_ref[0]
    segments = feat_ref.shape[0]
    rows = segments // LANES
    tiles = segments // RAYS_DEV
    per_tile = RAYS_DEV // LANES
    window = RAYS_DEV + ALIGN

    target = block_ref[...] ^ me
    onehot = jnp.concatenate([(target == d).astype(F32) for d in range(count)], axis=0)
    onehot_b = onehot.astype(BF16)
    upper = (iota((LANES, LANES), 0) <= iota((LANES, LANES), 1)).astype(F32).astype(BF16)
    within = dot(onehot_b, upper)
    total = dot(onehot_b, jnp.ones((LANES, LANES), BF16))
    size = count * rows
    r_i, c_i = iota((size, size), 0), iota((size, size), 1)
    first = r_i - lax.rem(r_i, rows)
    earlier = ((c_i < r_i) & (c_i >= first)).astype(F32).astype(BF16)
    start = dot(earlier, total.astype(BF16))
    position = within - 1.0 + start
    start_i = start.astype(I32)

    rank_t = jnp.transpose(rank_ref[...].astype(F32))
    ray_col = iota((RAYS_DEV, LANES), 0).astype(F32)
    odd = (iota((RAYS_DEV, LANES), 1) & 1) == 1
    slot_iota = iota((window, RAYS_DEV), 0).astype(F32)
    for d in range(count):
        packed[d, 0:ALIGN, :] = jnp.zeros((ALIGN, 2 * LANES), BF16)
    for j in range(tiles):
        rank_col = jnp.broadcast_to(rank_t[:, j : j + 1] + 1.0, (RAYS_DEV, LANES))
        extra = jnp.where(odd, rank_col, ray_col).astype(BF16)
        source = jnp.concatenate([feat_ref[j * RAYS_DEV : (j + 1) * RAYS_DEV, :], extra], axis=1)
        for d in range(count):
            row = d * rows + j * per_tile
            base_vec = start_i[row : row + 1, :] & (-ALIGN)
            base = pl.multiple_of(jnp.max(base_vec), ALIGN)
            base_f = base_vec.astype(F32)
            pieces = []
            for i in range(per_tile):
                hit = onehot[row + i : row + i + 1, :] > 0.5
                pieces.append(jnp.where(hit, position[row + i : row + i + 1, :] - base_f, -1.0))
            key = jnp.concatenate(pieces, axis=1)
            select = jnp.where(slot_iota == key, 1.0, 0.0).astype(BF16)
            moved = dot(select, source).astype(BF16)
            head = packed[d, pl.ds(base, ALIGN), :] + moved[:ALIGN]
            packed[d, pl.ds(base, ALIGN), :] = head
            packed[d, pl.ds(base + ALIGN, RAYS_DEV), :] = moved[ALIGN:]

    lane_pair = iota((capacity, LANES), 1) >> 1
    info = jnp.zeros((capacity, LANES), F32)
    valid_row = iota((capacity, LANES), 0)
    for d in range(count):
        last = d * rows + rows - 1
        filled = jnp.max((start + total)[last : last + 1, :].astype(I32))
        piece = packed[d, 0:capacity, LANES:].astype(F32)
        keep = (lane_pair == d) & (valid_row < filled)
        info = jnp.where(keep, piece, info)
        outs[d][0:capacity, :] = jnp.where(
            valid_row < filled, packed[d, 0:capacity, :LANES].astype(F32), 0.0
        ).astype(BF16)
    info_t = jnp.transpose(info)
    blocks = capacity // LANES
    mrows = meta_rows(capacity)
    for d in range(count):
        parts = []
        for which in range(2):
            line = info_t[2 * d + which : 2 * d + which + 1, :]
            parts += [line[:, i * LANES : (i + 1) * LANES] for i in range(blocks)]
            if mrows > blocks:
                parts.append(jnp.zeros((mrows - blocks, LANES), F32))
        outs[d][capacity:, :] = jnp.concatenate(parts, axis=0).astype(BF16)


def slot_lines(info, capacity):
    blocks = capacity // LANES
    mrows = meta_rows(capacity)
    ray = jnp.concatenate([info[i : i + 1, :] for i in range(blocks)], axis=1)
    rank = jnp.concatenate([info[mrows + i : mrows + i + 1, :] for i in range(blocks)], axis=1)
    return ray, rank


def mlp_kernel(capacity, tile, prior, *refs):
    message, w_in, w_hidden, w_out, w_dens = refs[:5]
    earlier = refs[5 : 5 + prior]
    feat_out, dens_out = refs[5 + prior : 7 + prior]
    hid = w_in.shape[1]
    layers = w_hidden.shape[0]
    tiles = capacity // tile
    acts = [
        silu(dot(message[i * tile : (i + 1) * tile, :], w_in[...])).astype(BF16)
        for i in range(tiles)
    ]
    for layer in range(layers):
        for i in range(tiles):
            update = silu(dot(acts[i], w_hidden[layer]))
            acts[i] = (acts[i].astype(F32) + update).astype(BF16)
    w_line = jnp.broadcast_to(w_dens[...].astype(F32), (8, hid)).astype(BF16)
    raws = [dot_nt(w_line, acts[i]) for i in range(tiles)]
    raw = jnp.concatenate(raws, axis=1)
    softplus = jnp.maximum(raw, 0.0) + jnp.log1p(jnp.exp(-jnp.abs(raw)))
    density = (0.25 * softplus).astype(BF16).astype(F32)
    ray, rank = slot_lines(message[capacity:, :].astype(F32), capacity)
    rank_hit = (rank - 1.0) == iota((SEGS_RAY, capacity), 0).astype(F32)
    by_rank = jnp.where(rank_hit, density[:SEGS_RAY], 0.0).astype(BF16)
    by_ray = jnp.where(iota((RAYS_DEV, capacity), 0).astype(F32) == ray, 1.0, 0.0).astype(BF16)
    table = dot_nt(by_rank, by_ray)
    parts = [e[...] for e in earlier] + [table]
    dens_out[...] = jnp.concatenate(parts, axis=0).astype(dens_out.dtype)
    for i in range(tiles):
        feat_out[i * tile : (i + 1) * tile, :] = dot(acts[i], w_out[...]).astype(BF16)


def color_kernel(count, capacity, me_ref, *refs):
    tables = refs[:count]
    feats = refs[count : 2 * count]
    infos = refs[2 * count : 3 * count]
    outs = refs[3 * count : 4 * count]
    edges = refs[4 * count]
    me = me_ref[0]
    size = count * SEGS_RAY
    summed = []
    for f in range(count):
        part = None
        for e in range(count):
            d = f ^ e
            rows = tables[e][d * SEGS_RAY : (d + 1) * SEGS_RAY, :].astype(F32)
            part = rows if part is None else part + rows
        summed.append(part)
    density = jnp.concatenate(summed, axis=0)
    r_i, c_i = iota((size, size), 0), iota((size, size), 1)
    first = r_i - lax.rem(r_i, SEGS_RAY)
    nearer = ((c_i < r_i) & (c_i >= first)).astype(F32).astype(BF16)
    optical = dot(nearer, density.astype(BF16))
    weight = jnp.exp(-optical) * (1.0 - jnp.exp(-density))
    high = weight.astype(BF16).astype(F32)
    low = weight - high
    e_r, e_c = iota((2 * EDGE, RAYS_DEV), 0), iota((2 * EDGE, RAYS_DEV), 1)
    second = (e_r >= EDGE).astype(I32)
    e_i = e_r - second * EDGE
    e_y = e_i // CONV_LAYERS
    e_x = lax.rem(e_i, CONV_LAYERS)
    ray_of = e_y * TW + jnp.where(second == 1, e_x, e_x + TW - CONV_LAYERS)
    pick = (ray_of == e_c).astype(F32).astype(BF16)
    zero_edge = jnp.zeros((2 * EDGE, LANES), BF16)
    edges[0] = zero_edge
    edges[count + 1] = zero_edge
    for f in range(count):
        ray, rank = slot_lines(infos[f][capacity:, :].astype(F32), capacity)
        rank_hit = jnp.where(
            (rank - 1.0) == iota((SEGS_RAY, capacity), 0).astype(F32), 1.0, 0.0
        )
        rank_hit = jnp.concatenate([rank_hit, rank_hit], axis=0).astype(BF16)
        rows = slice(f * SEGS_RAY, (f + 1) * SEGS_RAY)
        both = jnp.concatenate([high[rows], low[rows]], axis=0).astype(BF16)
        spread = dot_tn(both, rank_hit)
        ray_hit = iota((RAYS_DEV, capacity), 0).astype(F32) == ray
        mixing = jnp.where(ray_hit, spread, 0.0).astype(BF16)
        color = dot(mixing, feats[f][...]).astype(BF16)
        outs[f][0:RAYS_DEV, :] = color
        edges[(me ^ f) + 1] = dot(pick, color).astype(BF16)
    for f in range(count):
        place = me ^ f
        outs[f][RAYS_DEV : RAYS_DEV + EDGE, :] = edges[place, 0:EDGE, :]
        outs[f][RAYS_DEV + EDGE :, :] = edges[place + 2, EDGE:, :]


def sum_kernel(count, *refs):
    parts = refs[:count]
    tile_out, first_out, last_out = refs[count:]
    total = parts[0][...].astype(F32)
    for e in range(1, count):
        total = total + parts[e][...].astype(F32)
    tile = total.astype(BF16)
    tile_out[...] = tile
    edge = CONV_LAYERS * TW
    left, right = RAYS_DEV, RAYS_DEV + EDGE
    first_out[...] = jnp.concatenate(
        [tile[0:edge], tile[left : left + ALIGN], tile[right : right + ALIGN]], axis=0
    )
    last_out[...] = jnp.concatenate(
        [
            tile[RAYS_DEV - edge : RAYS_DEV],
            tile[left + EDGE - ALIGN : left + EDGE],
            tile[right + EDGE - ALIGN : right + EDGE],
        ],
        axis=0,
    )


PITCH = 2 * TW
TALL = TH + 2 * CONV_LAYERS


def conv_kernel(place_ref, tile_ref, above_ref, below_ref, w_ref, out_ref, image):
    row0, col0, rows_total, cols_total = (place_ref[i] for i in range(4))
    edge = CONV_LAYERS * TW
    left, right = RAYS_DEV, RAYS_DEV + EDGE
    pool = jnp.concatenate(
        [
            tile_ref[left : left + 2 * EDGE, :],
            above_ref[edge:, :],
            below_ref[edge:, :],
        ],
        axis=0,
    )
    strips = TALL + 1
    s_r, s_c = iota((strips * TW, pool.shape[0]), 0), iota((strips * TW, pool.shape[0]), 1)
    strip = s_r // TW
    sub = lax.rem(s_r, TW)
    is_right = sub < CONV_LAYERS
    is_left = sub >= TW - CONV_LAYERS
    y = jnp.where(is_left, strip - CONV_LAYERS, strip - 1 - CONV_LAYERS)
    i = jnp.where(is_left, sub - (TW - CONV_LAYERS), sub)
    side = jnp.where(is_left, 0, 1)
    inner = side * EDGE + y * CONV_LAYERS + i
    skip = ALIGN - CONV_LAYERS * CONV_LAYERS
    over = 2 * EDGE + side * ALIGN + skip + (y + CONV_LAYERS) * CONV_LAYERS + i
    under = 2 * EDGE + 2 * ALIGN + side * ALIGN + (y - TH) * CONV_LAYERS + i
    want = jnp.where(y < 0, over, jnp.where(y >= TH, under, inner))
    usable = (is_left | is_right) & (y >= -CONV_LAYERS) & (y < TH + CONV_LAYERS)
    want = jnp.where(usable, want, -1)
    place = (want == s_c).astype(F32).astype(BF16)
    borders = dot(place, pool).astype(BF16)
    zeros = jnp.zeros((TW, LANES), BF16)
    image[0:TW, :] = zeros
    for k in range(strips):
        at = k * PITCH + TW
        image[at : at + TW, :] = borders[k * TW : (k + 1) * TW]
        if k < TALL:
            y_k = k - CONV_LAYERS
            if y_k < 0:
                piece = above_ref[k * TW : (k + 1) * TW, :]
            elif y_k >= TH:
                piece = below_ref[(y_k - TH) * TW : (y_k - TH + 1) * TW, :]
            else:
                piece = tile_ref[y_k * TW : (y_k + 1) * TW, :]
            image[(k + 1) * PITCH : (k + 1) * PITCH + TW, :] = piece
    current = image[PITCH : PITCH + TALL * PITCH, :]
    head = image[PITCH - ALIGN : PITCH, :]
    current = jnp.concatenate([head, current], axis=0)
    height = TALL
    for layer in range(CONV_LAYERS):
        height = height - 2
        span = height * PITCH + ALIGN
        stacked = jnp.concatenate(
            [current[dy * PITCH : dy * PITCH + span] for dy in range(3)], axis=1
        )
        kernel = jnp.concatenate(
            [
                jnp.concatenate([w_ref[layer, dy, dx] for dx in range(3)], axis=1)
                for dy in range(3)
            ],
            axis=0,
        )
        full = dot(stacked, kernel)
        total = (
            pltpu.roll(full[:, :LANES], 1, 0)
            + full[:, LANES : 2 * LANES]
            + pltpu.roll(full[:, 2 * LANES :], span - 1, 0)
        )
        center = current[PITCH : PITCH + span].astype(F32)
        value = center + silu(total)
        at = iota((span, LANES), 0)
        y_at = at // PITCH
        x_at = lax.rem(at, PITCH) - TW
        upper = x_at < -(TW // 2)
        y_at = jnp.where(upper, y_at - 1, y_at)
        x_at = jnp.where(upper, x_at + PITCH, x_at)
        margin = CONV_LAYERS - 1 - layer
        y_img = row0 + y_at - margin
        x_img = col0 + x_at
        keep = (y_img >= 0) & (y_img < rows_total) & (x_img >= 0) & (x_img < cols_total)
        current = jnp.where(keep, value, 0.0).astype(BF16)
    for y_k in range(TH):
        at = ALIGN + y_k * PITCH
        out_ref[y_k * TW : (y_k + 1) * TW, :] = current[at : at + TW]


def shards(seg_feat, seg_block, depth_rank, w_in, w_hidden, w_out, w_dens, conv_w):
    count = lax.axis_size("blocks")
    segments, width = seg_feat.shape[2:]
    hid = w_in.shape[2]
    feat = w_out.shape[2]
    layers = w_hidden.shape[1]
    capacity = 2 * segments // count
    length = capacity + 2 * meta_rows(capacity)
    column = lax.axis_index("blocks").astype(I32)
    tile_row = lax.axis_index(("tiles", "sub")).astype(I32)
    me = column.reshape(1)
    smem = pl.BlockSpec(memory_space=pltpu.SMEM)
    vmem = pl.BlockSpec(memory_space=pltpu.VMEM)

    messages = pl.pallas_call(
        functools.partial(pack_kernel, count, capacity),
        out_shape=[jax.ShapeDtypeStruct((length, width), BF16)] * count,
        in_specs=[smem, vmem, vmem, vmem],
        out_specs=[vmem] * count,
        scratch_shapes=[
            pltpu.VMEM((count, capacity + RAYS_DEV + ALIGN, 2 * LANES), BF16)
        ],
        name="pack",
    )(me, seg_feat[0, 0], seg_block.reshape(segments // LANES, LANES), depth_rank[0, 0])

    def swap(value, d):
        return lax.ppermute(value, "blocks", [(i, i ^ d) for i in range(count)])

    received = {0: messages[0]}
    lag = 2
    order = [2, 1, 3] if count == 4 else list(range(1, count))
    for at, d in enumerate(order):
        value = messages[d]
        if at >= lag:
            ahead = order[at - lag]
            value, received[ahead] = lax.optimization_barrier((value, received[ahead]))
        received[d] = swap(value, d)

    sequence = [0, 1, 2, 3] if count == 4 else list(range(count))
    feats, tables = [], []
    flops = 2 * capacity * (width * hid + layers * hid * hid + hid * feat)
    for d in sequence:
        final = d == count - 1
        prior = count - 1 if final else 0
        height = count * SEGS_RAY if final else SEGS_RAY
        features, table = pl.pallas_call(
            functools.partial(mlp_kernel, capacity, min(capacity, 256), prior),
            out_shape=[
                jax.ShapeDtypeStruct((capacity, feat), BF16),
                jax.ShapeDtypeStruct((height, RAYS_DEV), BF16 if final else F32),
            ],
            in_specs=[vmem] * (5 + prior),
            out_specs=[vmem] * 2,
            cost_estimate=pl.CostEstimate(
                flops=flops, bytes_accessed=0, transcendentals=capacity * hid * (layers + 1)
            ),
            name="mlp",
        )(received[d], w_in[0], w_hidden[0], w_out[0], w_dens, *(tables if final else ()))
        feats.append(features)
        tables.append(table)
    local = tables[-1]
    others = [local] + [swap(local, d) for d in range(1, count)]

    height = RAYS_DEV + 2 * EDGE
    partial = pl.pallas_call(
        functools.partial(color_kernel, count, capacity),
        out_shape=[jax.ShapeDtypeStruct((height, feat), BF16)] * count,
        in_specs=[smem] + [vmem] * (3 * count),
        out_specs=[vmem] * count,
        scratch_shapes=[pltpu.VMEM((count + 2, 2 * EDGE, feat), BF16)],
        name="color",
    )(me, *others, *feats, *[received[d] for d in range(count)])
    pieces = [partial[0]] + [swap(partial[d], d) for d in range(1, count)]

    strip = CONV_LAYERS * TW + 2 * ALIGN
    tile, first, last = pl.pallas_call(
        functools.partial(sum_kernel, count),
        out_shape=[
            jax.ShapeDtypeStruct((height, feat), BF16),
            jax.ShapeDtypeStruct((strip, feat), BF16),
            jax.ShapeDtypeStruct((strip, feat), BF16),
        ],
        in_specs=[vmem] * count,
        out_specs=[vmem] * 3,
        name="total",
    )(*pieces)
    vertical = ("tiles", "sub")
    peers = lax.axis_size(vertical)
    above = lax.ppermute(last, vertical, [(i, i + 1) for i in range(peers - 1)])
    below = lax.ppermute(first, vertical, [(i + 1, i) for i in range(peers - 1)])

    where = jnp.stack(
        [tile_row * TH, column * TW, jnp.int32(TH * peers), jnp.int32(TW * count)]
    )
    decoded = pl.pallas_call(
        conv_kernel,
        out_shape=jax.ShapeDtypeStruct((RAYS_DEV, feat), BF16),
        in_specs=[smem] + [vmem] * 4,
        out_specs=vmem,
        scratch_shapes=[pltpu.VMEM(((TALL + 1) * PITCH + PITCH, feat), BF16)],
        name="decode",
    )(where, tile, above, below, conv_w)
    return decoded.reshape(TH, TW, feat)


def solution(mesh):
    in_specs = (
        P(("groups", "tiles", "sub"), "blocks", None, None),
        P(("groups", "tiles", "sub"), "blocks", None, None),
        P(("groups", "tiles", "sub"), "blocks", None, None),
        P("blocks", None, None),
        P("blocks", None, None, None),
        P("blocks", None, None),
        P("blocks", None),
        P(),
    )
    out_specs = P(("groups", "tiles", "sub"), "blocks", None)
    return jax.shard_map(shards, mesh=mesh, in_specs=in_specs, out_specs=out_specs, check_vma=False)
```

time: 132 us -> 82.6 us (0.63)
  Pallas kernels: 0 us -> 40.6 us
  blocking collectives: 30.1 us -> 0 us
  matrix products: 29.7 us -> 0 us
  local copies, waits for them, and re-layouts: 30.1 us -> 3.29 us
  starting transfers between devices: 17.9 us -> 25 us
  waiting for transfers between devices: 17.9 us -> 12.6 us
  other arithmetic: 4.93 us -> 0.67 us
    pallas_call x0 -> x8, Pallas kernels: none -> 40.6 us  [the longest x4 26.6 us: shards(): pl.pallas_call(functools.partial(mlp_kernel, capacity, min(capacity, 256)...]
    all_to_all x1 -> x0, blocking collectives: 30.1 us -> none  [shards(): lax.all_to_all(sendbuf, 'blocks', split_axis=0, concat_axis=0, tiled=True)]
    dot_general x10 -> x0, matrix products: 29.7 us -> none  [the longest x4 18.4 us: evaluate(): jnp.dot(hidden_act, hidden[layer_index], preferred_element_type=jnp.float32)]
    gather x2 -> x0, local copies, waits for them, and re-layouts: 19.3 us -> none  [the longest x1 13.1 us: shards(): density_back.reshape(block_count * capacity)[slot_index]]
    ppermute x4 -> x11, starting transfers between devices: 10 us -> 25 us  [the longest x9 15.8 us: swap(): return lax.ppermute(value, 'blocks', [(i, i ^ d) for i in range(count)])]
    all_to_all x2 -> x0, waiting for transfers between devices: 11.9 us -> none  [the longest x1 11.9 us: shards(): lax.all_to_all(features, 'blocks', split_axis=0, concat_axis=0, tiled=True)]
    all_to_all x2 -> x0, starting transfers between devices: 7.87 us -> none  [the longest x1 4.44 us: shards(): lax.all_to_all(features, 'blocks', split_axis=0, concat_axis=0, tiled=True)]
    ppermute x4 -> x11, waiting for transfers between devices: 6 us -> 12.6 us  [the longest x9 9.9 us: swap(): return lax.ppermute(value, 'blocks', [(i, i ^ d) for i in range(count)])]
  transfers between devices with their start and end apart: 6 -> 11, of which waited for: 3 -> 6; matrix products, arithmetic and copies ran while one was open for 14% -> 1% of each run, Pallas kernels for 0% -> 24%
where the time goes in v1:
time: 82.6 us; the launch traced here: 82.2 us
  Pallas kernels  40.6 us (49%)
  starting transfers between devices  25 us (30%)
  waiting for transfers between devices  12.6 us (15%)
  local copies, waits for them, and re-layouts  3.29 us (4%)
    pallas_call x4, Pallas kernels, shards(): pl.pallas_call(functools.partial(mlp_kernel, capacity, min(capacity, 256)...  26.6 us
    ppermute x9, starting transfers between devices, swap(): return lax.ppermute(value, 'blocks', [(i, i ^ d) for i in range(count)])  15.8 us
    ppermute x9, waiting for transfers between devices, swap(): return lax.ppermute(value, 'blocks', [(i, i ^ d) for i in range(count)])  9.9 us
    ppermute x1, starting transfers between devices, shards(): above = lax.ppermute(last, vertical, [(i, i + 1) for i in range(peers - 1)])  7.3 us
    pallas_call x1, Pallas kernels, shards(): pl.pallas_call(functools.partial(pack_kernel, count, capacity), out_shape...  4.45 us
    pallas_call x1, Pallas kernels, shards(): pl.pallas_call(functools.partial(color_kernel, count, capacity), out_shap...  4.29 us
    pallas_call x1, Pallas kernels, shards(): pl.pallas_call(conv_kernel, out_shape=jax.ShapeDtypeStruct((RAYS_DEV, fea...  3.61 us
    unnamed x24, local copies, waits for them, and re-layouts  3.28 us
  transfers between devices with their start and end apart: 11, of which 6 were waited for; matrix products, arithmetic and copies ran while one was open for 1% of the time, Pallas kernels for 24%

profile of v1, /device:TPU:1, one launch (start us, length us, event | category | flops | bytes accessed | tf_op | source)
XLA Modules:
  0.0 82.2 jit_solution(7647465114613302009)
XLA Ops:
  0.0 4.4 %pack.1 = (bf16[1040,128]{1,0:T(8,128)(2,1)}, bf16[1040,128]{1,0:T(8,128)(2,1)}, bf16[1040,128]{1,0:T(8,128)(2,1)}, bf16[1040,128]{1,0:T(8,128)(2,1)}) custom-call(s32[1]{0:T(128)} %bitcast.2.me_ref, bf16[2048,128]{1,0:T(8,128)(2,1)} %bitcast.10, s32[16,128]{1,0:T(8,128)} %bitcast.11, s32[8,256]{1,0:T(8,128)} %bitcast.12), custom_call_target="tpu_custom_call" | custom-call | tf_op jit(solution)/shard_map/pack/pallas_call | solution.py:342
  4.4 3.1 %collective-permute-start = (bf16[1040,128]{1,0:T(8,128)(2,1)}, bf16[1040,128]{1,0:T(8,128)(2,1)S(1)}, u32[]{:S(2)}, u32[]{:S(2)}) collective-permute-start(bf16[1040,128]{1,0:T(8,128)(2,1)} %get-tuple-element.27), channel_id=1, source_target_pairs={{0,8},{4,12},{8,0},{12,4},{1,9},{5,13},{9,1},{13,5},{2,10},{6,14},... | collective-permute-start | bytes 798728 | tf_op jit(solution)/shard_map/ppermute | solution.py:354
  7.6 1.3 %collective-permute-start.2 = (bf16[1040,128]{1,0:T(8,128)(2,1)}, bf16[1040,128]{1,0:T(8,128)(2,1)S(1)}, u32[]{:S(2)}, u32[]{:S(2)}) collective-permute-start(bf16[1040,128]{1,0:T(8,128)(2,1)} %get-tuple-element.31), channel_id=1, source_target_pairs={{0,4},{4,0},{8,12},{12,8},{1,5},{5,1},{9,13},{13,9},{2,6},{6,2},{1... | collective-permute-start | bytes 798728 | tf_op jit(solution)/shard_map/ppermute | solution.py:354
  8.9 0.0 copy-start.11
  8.9 6.6 %mlp.4 = (bf16[1024,128]{1,0:T(8,128)(2,1)}, f32[8,256]{1,0:T(8,128)}) custom-call(bf16[1040,128]{1,0:T(8,128)(2,1)} %get-tuple-element.29.refs_0_.refs_8_, bf16[128,512]{1,0:T(8,128)(2,1)} %bitcast.17, bf16[4,512,512]{2,1,0:T(8,128)(2,1)} %bitcast.13, bf16[512,128]{1,0:T(8,128)(2,1)} %bitcast.21, bf16[1,512]{1,0:T(2,128)(2,1)} %refs_4_.7), custom_call_target="tpu_custom_call" | custom-call | flops 2415919104 | tf_op jit(solution)/shard_map/mlp/pallas_call | solution.py:373
  15.5 4.2 %collective-permute-done.refs_0_.refs_10_ = bf16[1040,128]{1,0:T(8,128)(2,1)S(1)} collective-permute-done((bf16[1040,128]{1,0:T(8,128)(2,1)}, bf16[1040,128]{1,0:T(8,128)(2,1)S(1)}, u32[]{:S(2)}, u32[]{:S(2)}) %collective-permute-start) | collective-permute-done | bytes 266272 | tf_op jit(solution)/shard_map/ppermute | solution.py:354
  19.6 0.0 copy-start
  19.6 0.0 copy-done.11
  19.6 4.0 %collective-permute-start.1 = (bf16[1040,128]{1,0:T(8,128)(2,1)S(1)}, bf16[1040,128]{1,0:T(8,128)(2,1)S(1)}, u32[]{:S(2)}, u32[]{:S(2)}) collective-permute-start(bf16[1040,128]{1,0:T(8,128)(2,1)S(1)} %copy-done.11), channel_id=1, source_target_pairs={{0,12},{4,8},{8,4},{12,0},{1,13},{5,9},{9,5},{13,1},{2,14},{6,10},... | collective-permute-start | bytes 798728 | tf_op jit(solution)/shard_map/ppermute | solution.py:354
  23.6 0.0 copy-done
  23.6 6.6 %mlp.6 = (bf16[1024,128]{1,0:T(8,128)(2,1)}, f32[8,256]{1,0:T(8,128)}) custom-call(bf16[1040,128]{1,0:T(8,128)(2,1)} %copy-done, bf16[128,512]{1,0:T(8,128)(2,1)} %bitcast.18, bf16[4,512,512]{2,1,0:T(8,128)(2,1)} %bitcast.14, bf16[512,128]{1,0:T(8,128)(2,1)} %bitcast.22, bf16[1,512]{1,0:T(2,128)(2,1)} %refs_4_.7), custom_call_target="tpu_custom_call" | custom-call | flops 2415919104 | tf_op jit(solution)/shard_map/mlp/pallas_call | solution.py:373
  30.2 0.0 collective-permute-done.2.refs_0_.refs_9_
  30.2 0.0 copy-start.1
  30.2 0.7 copy-done.1
  30.9 6.8 %mlp.5 = (bf16[1024,128]{1,0:T(8,128)(2,1)}, f32[8,256]{1,0:T(8,128)}) custom-call(bf16[1040,128]{1,0:T(8,128)(2,1)} %copy-done.1, bf16[128,512]{1,0:T(8,128)(2,1)} %bitcast.19, bf16[4,512,512]{2,1,0:T(8,128)(2,1)} %bitcast.15, bf16[512,128]{1,0:T(8,128)(2,1)} %bitcast.23, bf16[1,512]{1,0:T(2,128)(2,1)} %refs_4_.7), custom_call_target="tpu_custom_call" | custom-call | flops 2415919104 | tf_op jit(solution)/shard_map/mlp/pallas_call | solution.py:373
  37.7 0.0 collective-permute-done.1.refs_0_.refs_11_
  37.7 0.0 copy-start.2
  37.7 0.7 copy-done.2
  38.4 6.6 %mlp.7 = (bf16[1024,128]{1,0:T(8,128)(2,1)}, bf16[32,256]{1,0:T(8,128)(2,1)}) custom-call(bf16[1040,128]{1,0:T(8,128)(2,1)} %copy-done.2, bf16[128,512]{1,0:T(8,128)(2,1)} %bitcast.20, bf16[4,512,512]{2,1,0:T(8,128)(2,1)} %bitcast.16, bf16[512,128]{1,0:T(8,128)(2,1)} %bitcast.24, bf16[1,512]{1,0:T(2,128)(2,1)} %refs_4_.7, ...), custom_call_target="tpu_custom_call" | custom-call | flops 2415919104 | tf_op jit(solution)/shard_map/mlp/pallas_call | solution.py:373
  45.0 0.7 collective-permute-start.5
  45.7 0.0 collective-permute-start.4
  45.7 2.8 %collective-permute-start.3 = (bf16[32,256]{1,0:T(8,128)(2,1)}, bf16[32,256]{1,0:T(8,128)(2,1)S(1)}, u32[]{:S(2)}, u32[]{:S(2)}) collective-permute-start(bf16[32,256]{1,0:T(8,128)(2,1)} %get-tuple-element.35.refs_0_), channel_id=1, source_target_pairs={{0,4},{4,0},{8,12},{12,8},{1,5},{5,1},{9,13},{13,9},{2,6},{6,2},{1... | collective-permute-start | bytes 49160 | tf_op jit(solution)/shard_map/ppermute | solution.py:354
  48.6 1.0 %collective-permute-done.5.refs_3_ = bf16[32,256]{1,0:T(8,128)(2,1)S(1)} collective-permute-done((bf16[32,256]{1,0:T(8,128)(2,1)}, bf16[32,256]{1,0:T(8,128)(2,1)S(1)}, u32[]{:S(2)}, u32[]{:S(2)}) %collective-permute-start.5) | collective-permute-done | bytes 16416 | tf_op jit(solution)/shard_map/ppermute | solution.py:354
  49.6 0.0 copy-start.8
  49.6 0.0 collective-permute-done.4.refs_2_
  49.6 0.0 copy-start.9
  49.6 0.3 collective-permute-done.3.refs_1_
  49.9 0.0 copy-start.10
  49.9 0.3 copy-done.8
  50.2 0.0 copy-done.9
  50.2 0.3 copy-done.10
  50.5 4.3 %color.1 = (bf16[352,128]{1,0:T(8,128)(2,1)}, bf16[352,128]{1,0:T(8,128)(2,1)}, bf16[352,128]{1,0:T(8,128)(2,1)}, bf16[352,128]{1,0:T(8,128)(2,1)}) custom-call(s32[1]{0:T(128)} %bitcast.2.me_ref, bf16[32,256]{1,0:T(8,128)(2,1)} %get-tuple-element.35.refs_0_, bf16[32,256]{1,0:T(8,128)(2,1)} %copy-done.10, bf16[32,256]{1,0:T(8,128)(2,1)} %copy-done.9, ...), custom_call_target="tpu_custom_call" | custom-call | tf_op jit(solution)/shard_map/color/pallas_call | solution.py:392
  54.8 1.7 %collective-permute-start.6 = (bf16[352,128]{1,0:T(8,128)(2,1)}, bf16[352,128]{1,0:T(8,128)(2,1)S(1)}, u32[]{:S(2)}, u32[]{:S(2)}) collective-permute-start(bf16[352,128]{1,0:T(8,128)(2,1)} %get-tuple-element.41), channel_id=1, source_target_pairs={{0,4},{4,0},{8,12},{12,8},{1,5},{5,1},{9,13},{13,9},{2,6},{6,2},{1... | collective-permute-start | bytes 270344 | tf_op jit(solution)/shard_map/ppermute | solution.py:354
  56.5 0.7 collective-permute-start.7
  57.2 1.5 %collective-permute-start.8 = (bf16[352,128]{1,0:T(8,128)(2,1)}, bf16[352,128]{1,0:T(8,128)(2,1)S(1)}, u32[]{:S(2)}, u32[]{:S(2)}) collective-permute-start(bf16[352,128]{1,0:T(8,128)(2,1)} %get-tuple-element.43), channel_id=1, source_target_pairs={{0,12},{4,8},{8,4},{12,0},{1,13},{5,9},{9,5},{13,1},{2,14},{6,10},... | collective-permute-start | bytes 270344 | tf_op jit(solution)/shard_map/ppermute | solution.py:354
  58.7 0.0 collective-permute-done.6.refs_1_
  58.7 0.0 copy-start.3
  58.7 3.3 %collective-permute-done.7.refs_2_ = bf16[352,128]{1,0:T(8,128)(2,1)S(1)} collective-permute-done((bf16[352,128]{1,0:T(8,128)(2,1)}, bf16[352,128]{1,0:T(8,128)(2,1)S(1)}, u32[]{:S(2)}, u32[]{:S(2)}) %collective-permute-start.7) | collective-permute-done | bytes 90144 | tf_op jit(solution)/shard_map/ppermute | solution.py:354
  62.0 0.0 copy-start.4
  62.0 1.1 %collective-permute-done.8.refs_3_ = bf16[352,128]{1,0:T(8,128)(2,1)S(1)} collective-permute-done((bf16[352,128]{1,0:T(8,128)(2,1)}, bf16[352,128]{1,0:T(8,128)(2,1)S(1)}, u32[]{:S(2)}, u32[]{:S(2)}) %collective-permute-start.8) | collective-permute-done | bytes 90144 | tf_op jit(solution)/shard_map/ppermute | solution.py:354
  63.0 0.0 copy-start.5
  63.0 0.0 copy-done.3
  63.0 0.0 copy-done.4
  63.0 0.6 copy-done.5
  63.7 1.7 %total.1 = (bf16[352,128]{1,0:T(8,128)(2,1)}, bf16[80,128]{1,0:T(8,128)(2,1)}, bf16[80,128]{1,0:T(8,128)(2,1)}) custom-call(bf16[352,128]{1,0:T(8,128)(2,1)} %get-tuple-element.40.refs_0_, bf16[352,128]{1,0:T(8,128)(2,1)} %copy-done.3, bf16[352,128]{1,0:T(8,128)(2,1)} %copy-done.4, bf16[352,128]{1,0:T(8,128)(2,1)} %copy-done.5), custom_call_target="tpu_custom_call" | custom-call | tf_op jit(solution)/shard_map/total/pallas_call | solution.py:403
  65.4 7.3 %collective-permute-start.9 = (bf16[80,128]{1,0:T(8,128)(2,1)}, bf16[80,128]{1,0:T(8,128)(2,1)S(1)}, u32[]{:S(2)}, u32[]{:S(2)}) collective-permute-start(bf16[80,128]{1,0:T(8,128)(2,1)} %get-tuple-element.45), channel_id=1, source_target_pairs={{0,1},{1,2},{2,3},{4,5},{5,6},{6,7},{8,9},{9,10},{10,11},{12,13},{... | collective-permute-start | bytes 61448 | tf_op jit(solution)/shard_map/ppermute | solution.py:416
  72.7 1.9 %collective-permute-start.10 = (bf16[80,128]{1,0:T(8,128)(2,1)}, bf16[80,128]{1,0:T(8,128)(2,1)S(1)}, u32[]{:S(2)}, u32[]{:S(2)}) collective-permute-start(bf16[80,128]{1,0:T(8,128)(2,1)} %get-tuple-element.46), channel_id=1, source_target_pairs={{1,0},{2,1},{3,2},{5,4},{6,5},{7,6},{9,8},{10,9},{11,10},{13,12},{... | collective-permute-start | bytes 61448 | tf_op jit(solution)/shard_map/ppermute | solution.py:417
  74.6 0.7 pad_add_fusion.place_ref
  75.3 0.0 collective-permute-done.9.above_ref
  75.3 0.0 copy-start.6
  75.3 2.7 %collective-permute-done.10.below_ref = bf16[80,128]{1,0:T(8,128)(2,1)S(1)} collective-permute-done((bf16[80,128]{1,0:T(8,128)(2,1)}, bf16[80,128]{1,0:T(8,128)(2,1)S(1)}, u32[]{:S(2)}, u32[]{:S(2)}) %collective-permute-start.10) | collective-permute-done | bytes 20512 | tf_op jit(solution)/shard_map/ppermute | solution.py:417
  78.0 0.0 copy-start.7
  78.0 0.0 copy-done.6
  78.0 0.6 copy-done.7
  78.6 3.6 %decode.1 = bf16[256,128]{1,0:T(8,128)(2,1)} custom-call(s32[4]{0:T(128)} %pad_add_fusion.place_ref, bf16[352,128]{1,0:T(8,128)(2,1)} %get-tuple-element.44.tile_ref, bf16[80,128]{1,0:T(8,128)(2,1)} %copy-done.6, bf16[80,128]{1,0:T(8,128)(2,1)} %copy-done.7, bf16[3,3,3,128,128]{4,3,2,1,0:T(8,128)(2,1)} %w_ref.1), custom_call_target="tpu_custom_call" | custom-call | tf_op jit(solution)/shard_map/decode/pallas_call | solution.py:422
  (1 shorter events, 0.0 us)
Async XLA Ops:
  4.4 15.2 %collective-permute-start = (bf16[1040,128]{1,0:T(8,128)(2,1)}, bf16[1040,128]{1,0:T(8,128)(2,1)S(1)}, u32[]{:S(2)}, u32[]{:S(2)}) collective-permute-start(bf16[1040,128]{1,0:T(8,128)(2,1)} %get-tuple-element.27), channel_id=1, source_target_pairs={{0,8},{4,12},{8,0},{12,4},{1,9},{5,13},{9,1},{13,5},{2,10},{6,14},... | collective-permute-start | bytes 798728 | tf_op jit(solution)/shard_map/ppermute | solution.py:354
  7.6 22.6 %collective-permute-start.2 = (bf16[1040,128]{1,0:T(8,128)(2,1)}, bf16[1040,128]{1,0:T(8,128)(2,1)S(1)}, u32[]{:S(2)}, u32[]{:S(2)}) collective-permute-start(bf16[1040,128]{1,0:T(8,128)(2,1)} %get-tuple-element.31), channel_id=1, source_target_pairs={{0,4},{4,0},{8,12},{12,8},{1,5},{5,1},{9,13},{13,9},{2,6},{6,2},{1... | collective-permute-start | bytes 798728 | tf_op jit(solution)/shard_map/ppermute | solution.py:354
  8.9 10.8 %copy-start.11 = (bf16[1040,128]{1,0:T(8,128)(2,1)S(1)}, bf16[1040,128]{1,0:T(8,128)(2,1)}, u32[]{:S(2)}) copy-start(bf16[1040,128]{1,0:T(8,128)(2,1)} %get-tuple-element.28) | copy-start | bytes 798724
  19.6 4.0 %copy-start = (bf16[1040,128]{1,0:T(8,128)(2,1)}, bf16[1040,128]{1,0:T(8,128)(2,1)S(1)}, u32[]{:S(2)}) copy-start(bf16[1040,128]{1,0:T(8,128)(2,1)S(1)} %collective-permute-done.refs_0_.refs_10_) | copy-start | bytes 798724
  19.6 18.1 %collective-permute-start.1 = (bf16[1040,128]{1,0:T(8,128)(2,1)S(1)}, bf16[1040,128]{1,0:T(8,128)(2,1)S(1)}, u32[]{:S(2)}, u32[]{:S(2)}) collective-permute-start(bf16[1040,128]{1,0:T(8,128)(2,1)S(1)} %copy-done.11), channel_id=1, source_target_pairs={{0,12},{4,8},{8,4},{12,0},{1,13},{5,9},{9,5},{13,1},{2,14},{6,10},... | collective-permute-start | bytes 798728 | tf_op jit(solution)/shard_map/ppermute | solution.py:354
  30.2 0.7 copy-start.1
  37.7 0.7 copy-start.2
  45.0 4.6 %collective-permute-start.5 = (bf16[32,256]{1,0:T(8,128)(2,1)}, bf16[32,256]{1,0:T(8,128)(2,1)S(1)}, u32[]{:S(2)}, u32[]{:S(2)}) collective-permute-start(bf16[32,256]{1,0:T(8,128)(2,1)} %get-tuple-element.35.refs_0_), channel_id=1, source_target_pairs={{0,12},{4,8},{8,4},{12,0},{1,13},{5,9},{9,5},{13,1},{2,14},{6,10},... | collective-permute-start | bytes 49160 | tf_op jit(solution)/shard_map/ppermute | solution.py:354
  45.7 3.9 %collective-permute-start.4 = (bf16[32,256]{1,0:T(8,128)(2,1)}, bf16[32,256]{1,0:T(8,128)(2,1)S(1)}, u32[]{:S(2)}, u32[]{:S(2)}) collective-permute-start(bf16[32,256]{1,0:T(8,128)(2,1)} %get-tuple-element.35.refs_0_), channel_id=1, source_target_pairs={{0,8},{4,12},{8,0},{12,4},{1,9},{5,13},{9,1},{13,5},{2,10},{6,14},... | collective-permute-start | bytes 49160 | tf_op jit(solution)/shard_map/ppermute | solution.py:354
  45.7 4.2 %collective-permute-start.3 = (bf16[32,256]{1,0:T(8,128)(2,1)}, bf16[32,256]{1,0:T(8,128)(2,1)S(1)}, u32[]{:S(2)}, u32[]{:S(2)}) collective-permute-start(bf16[32,256]{1,0:T(8,128)(2,1)} %get-tuple-element.35.refs_0_), channel_id=1, source_target_pairs={{0,4},{4,0},{8,12},{12,8},{1,5},{5,1},{9,13},{13,9},{2,6},{6,2},{1... | collective-permute-start | bytes 49160 | tf_op jit(solution)/shard_map/ppermute | solution.py:354
  49.6 0.6 copy-start.8
  49.6 0.6 copy-start.9
  49.9 0.6 copy-start.10
  54.8 3.8 %collective-permute-start.6 = (bf16[352,128]{1,0:T(8,128)(2,1)}, bf16[352,128]{1,0:T(8,128)(2,1)S(1)}, u32[]{:S(2)}, u32[]{:S(2)}) collective-permute-start(bf16[352,128]{1,0:T(8,128)(2,1)} %get-tuple-element.41), channel_id=1, source_target_pairs={{0,4},{4,0},{8,12},{12,8},{1,5},{5,1},{9,13},{13,9},{2,6},{6,2},{1... | collective-permute-start | bytes 270344 | tf_op jit(solution)/shard_map/ppermute | solution.py:354
  56.5 5.5 %collective-permute-start.7 = (bf16[352,128]{1,0:T(8,128)(2,1)}, bf16[352,128]{1,0:T(8,128)(2,1)S(1)}, u32[]{:S(2)}, u32[]{:S(2)}) collective-permute-start(bf16[352,128]{1,0:T(8,128)(2,1)} %get-tuple-element.42), channel_id=1, source_target_pairs={{0,8},{4,12},{8,0},{12,4},{1,9},{5,13},{9,1},{13,5},{2,10},{6,14},... | collective-permute-start | bytes 270344 | tf_op jit(solution)/shard_map/ppermute | solution.py:354
  57.2 5.9 %collective-permute-start.8 = (bf16[352,128]{1,0:T(8,128)(2,1)}, bf16[352,128]{1,0:T(8,128)(2,1)S(1)}, u32[]{:S(2)}, u32[]{:S(2)}) collective-permute-start(bf16[352,128]{1,0:T(8,128)(2,1)} %get-tuple-element.43), channel_id=1, source_target_pairs={{0,12},{4,8},{8,4},{12,0},{1,13},{5,9},{9,5},{13,1},{2,14},{6,10},... | collective-permute-start | bytes 270344 | tf_op jit(solution)/shard_map/ppermute | solution.py:354
  58.7 4.4 %copy-start.3 = (bf16[352,128]{1,0:T(8,128)(2,1)}, bf16[352,128]{1,0:T(8,128)(2,1)S(1)}, u32[]{:S(2)}) copy-start(bf16[352,128]{1,0:T(8,128)(2,1)S(1)} %collective-permute-done.6.refs_1_) | copy-start | bytes 270340
  62.0 1.1 %copy-start.4 = (bf16[352,128]{1,0:T(8,128)(2,1)}, bf16[352,128]{1,0:T(8,128)(2,1)S(1)}, u32[]{:S(2)}) copy-start(bf16[352,128]{1,0:T(8,128)(2,1)S(1)} %collective-permute-done.7.refs_2_) | copy-start | bytes 270340
  63.0 0.6 copy-start.5
  65.4 9.9 %collective-permute-start.9 = (bf16[80,128]{1,0:T(8,128)(2,1)}, bf16[80,128]{1,0:T(8,128)(2,1)S(1)}, u32[]{:S(2)}, u32[]{:S(2)}) collective-permute-start(bf16[80,128]{1,0:T(8,128)(2,1)} %get-tuple-element.45), channel_id=1, source_target_pairs={{0,1},{1,2},{2,3},{4,5},{5,6},{6,7},{8,9},{9,10},{10,11},{12,13},{... | collective-permute-start | bytes 61448 | tf_op jit(solution)/shard_map/ppermute | solution.py:416
  72.7 5.3 %collective-permute-start.10 = (bf16[80,128]{1,0:T(8,128)(2,1)}, bf16[80,128]{1,0:T(8,128)(2,1)S(1)}, u32[]{:S(2)}, u32[]{:S(2)}) collective-permute-start(bf16[80,128]{1,0:T(8,128)(2,1)} %get-tuple-element.46), channel_id=1, source_target_pairs={{1,0},{2,1},{3,2},{5,4},{6,5},{7,6},{9,8},{10,9},{11,10},{13,12},{... | collective-permute-start | bytes 61448 | tf_op jit(solution)/shard_map/ppermute | solution.py:417
  75.3 2.7 %copy-start.6 = (bf16[80,128]{1,0:T(8,128)(2,1)}, bf16[80,128]{1,0:T(8,128)(2,1)S(1)}, u32[]{:S(2)}) copy-start(bf16[80,128]{1,0:T(8,128)(2,1)S(1)} %collective-permute-done.9.above_ref) | copy-start | bytes 61444
  78.0 0.6 copy-start.7

commit v2 on v1

--- a/solution.py
+++ b/solution.py
@@ -40,6 +40,10 @@
 def silu(x):
     z = 0.5 * x
     return z + z * jnp.tanh(z)
+
+
+def grant(mib):
+    return pltpu.CompilerParams(vmem_limit_bytes=mib << 20)
 
 
 def meta_rows(capacity):
@@ -347,6 +351,7 @@
         scratch_shapes=[
             pltpu.VMEM((count, capacity + RAYS_DEV + ALIGN, 2 * LANES), BF16)
         ],
+        compiler_params=grant(10),
         name="pack",
     )(me, seg_feat[0, 0], seg_block.reshape(segments // LANES, LANES), depth_rank[0, 0])
 
@@ -381,7 +386,8 @@
             cost_estimate=pl.CostEstimate(
                 flops=flops, bytes_accessed=0, transcendentals=capacity * hid * (layers + 1)
             ),
-            name="mlp",
+            compiler_params=grant(14),
+        name="mlp",
         )(received[d], w_in[0], w_hidden[0], w_out[0], w_dens, *(tables if final else ()))
         feats.append(features)
         tables.append(table)
@@ -395,6 +401,7 @@
         in_specs=[smem] + [vmem] * (3 * count),
         out_specs=[vmem] * count,
         scratch_shapes=[pltpu.VMEM((count + 2, 2 * EDGE, feat), BF16)],
+        compiler_params=grant(12),
         name="color",
     )(me, *others, *feats, *[received[d] for d in range(count)])
     pieces = [partial[0]] + [swap(partial[d], d) for d in range(1, count)]
@@ -409,6 +416,7 @@
         ],
         in_specs=[vmem] * count,
         out_specs=[vmem] * 3,
+        compiler_params=grant(4),
         name="total",
     )(*pieces)
     vertical = ("tiles", "sub")
@@ -425,6 +433,7 @@
         in_specs=[smem] + [vmem] * 4,
         out_specs=vmem,
         scratch_shapes=[pltpu.VMEM(((TALL + 1) * PITCH + PITCH, feat), BF16)],
+        compiler_params=grant(8),
         name="decode",
     )(where, tile, above, below, conv_w)
     return decoded.reshape(TH, TW, feat)

time: 82.6 us -> 66.8 us (0.81)
  Pallas kernels: 40.6 us -> 23.9 us
  local copies, waits for them, and re-layouts: 3.29 us -> 6.54 us
  waiting for transfers between devices: 12.6 us -> 11.5 us
    pallas_call x4, Pallas kernels: 26.6 us -> 16.7 us  [shards(): pl.pallas_call(functools.partial(mlp_kernel, capacity, min(capacity, 256)...]
    unnamed x24 -> x22, local copies, waits for them, and re-layouts: 3.28 us -> 6.53 us
    pallas_call x1, Pallas kernels: 4.29 us -> 2 us  [shards(): pl.pallas_call(functools.partial(color_kernel, count, capacity), out_shap...]
    pallas_call x1, Pallas kernels: 4.45 us -> 2.31 us  [shards(): pl.pallas_call(functools.partial(pack_kernel, count, capacity), out_shape...]
    pallas_call x1, Pallas kernels: 1.7 us -> 0.05 us  [shards(): pl.pallas_call(functools.partial(sum_kernel, count), out_shape=[jax.Shape...]
    ppermute x9, waiting for transfers between devices: 9.9 us -> 8.46 us  [swap(): return lax.ppermute(value, 'blocks', [(i, i ^ d) for i in range(count)])]
  transfers between devices with their start and end apart: 11 -> 11, of which waited for: 6 -> 7; matrix products, arithmetic and copies ran while one was open for 1% -> 0% of each run, Pallas kernels for 24% -> 19%
where the time goes in v2:
time: 66.8 us; the launch traced here: 66.4 us
  starting transfers between devices  24.2 us (36%)
  Pallas kernels  23.9 us (36%)
  waiting for transfers between devices  11.5 us (17%)
  local copies, waits for them, and re-layouts  6.54 us (10%)
    pallas_call x4, Pallas kernels, shards(): pl.pallas_call(functools.partial(mlp_kernel, capacity, min(capacity, 256)...  16.7 us
    ppermute x9, starting transfers between devices, swap(): return lax.ppermute(value, 'blocks', [(i, i ^ d) for i in range(count)])  15.7 us
    ppermute x9, waiting for transfers between devices, swap(): return lax.ppermute(value, 'blocks', [(i, i ^ d) for i in range(count)])  8.46 us
    ppermute x1, starting transfers between devices, shards(): above = lax.ppermute(last, vertical, [(i, i + 1) for i in range(peers - 1)])  6.56 us
    unnamed x22, local copies, waits for them, and re-layouts  6.53 us
    ppermute x1, waiting for transfers between devices, shards(): lax.ppermute(first, vertical, [(i + 1, i) for i in range(peers - 1)])  3.08 us
    pallas_call x1, Pallas kernels, shards(): pl.pallas_call(conv_kernel, out_shape=jax.ShapeDtypeStruct((RAYS_DEV, fea...  2.9 us
    pallas_call x1, Pallas kernels, shards(): pl.pallas_call(functools.partial(pack_kernel, count, capacity), out_shape...  2.31 us
  transfers between devices with their start and end apart: 11, of which 7 were waited for; matrix products, arithmetic and copies ran while one was open for 0% of the time, Pallas kernels for 19%

profile of v2, /device:TPU:1, one launch (start us, length us, event | category | flops | bytes accessed | tf_op | source)
XLA Modules:
  0.0 66.4 jit_solution(2411031333480509642)
XLA Ops:
  0.0 0.0 copy-start.1
  0.0 1.0 %copy-done.1 = bf16[1,1,2048,128]{3,2,1,0:T(8,128)(2,1)S(1)} copy-done((bf16[1,1,2048,128]{3,2,1,0:T(8,128)(2,1)S(1)}, bf16[1,1,2048,128]{3,2,1,0:T(8,128)(2,1)}, u32[]{:S(2)}) %copy-start.1) | copy-done | bytes 524312
  1.0 0.0 copy-start.2
  1.0 0.7 %copy-done.2 = s32[1,1,2048,1]{2,3,1,0:T(1,128)S(1)} copy-done((s32[1,1,2048,1]{2,3,1,0:T(1,128)S(1)}, s32[1,1,2048,1]{2,3,1,0:T(1,128)}, u32[]{:S(2)}) %copy-start.2) | copy-done | bytes 8216
  1.7 0.0 copy-start.3
  1.7 0.7 %copy-done.3 = s32[1,1,8,256]{3,2,1,0:T(8,128)S(1)} copy-done((s32[1,1,8,256]{3,2,1,0:T(8,128)S(1)}, s32[1,1,8,256]{3,2,1,0:T(8,128)}, u32[]{:S(2)}) %copy-start.3) | copy-done | bytes 8216
  2.4 2.3 %pack.1 = (bf16[1040,128]{1,0:T(8,128)(2,1)S(1)}, bf16[1040,128]{1,0:T(8,128)(2,1)S(1)}, bf16[1040,128]{1,0:T(8,128)(2,1)S(1)}, bf16[1040,128]{1,0:T(8,128)(2,1)S(1)}) custom-call(s32[1]{0:T(128)} %bitcast.2.me_ref, bf16[2048,128]{1,0:T(8,128)(2,1)S(1)} %bitcast.10, s32[16,128]{1,0:T(8,128)S(1)} %bitcast.11, s32[8,256]{1,0:T(8,128)S(1)} %bitcast.12), custom_call_target="tpu_custom_call" | custom-call | tf_op jit(solution)/shard_map/pack/pallas_call | solution.py:346
  4.8 3.2 %collective-permute-start = (bf16[1040,128]{1,0:T(8,128)(2,1)S(1)}, bf16[1040,128]{1,0:T(8,128)(2,1)S(1)}, u32[]{:S(2)}, u32[]{:S(2)}) collective-permute-start(bf16[1040,128]{1,0:T(8,128)(2,1)S(1)} %get-tuple-element.27), channel_id=1, source_target_pairs={{0,8},{4,12},{8,0},{12,4},{1,9},{5,13},{9,1},{13,5},{2,10},{6,14},... | collective-permute-start | bytes 798728 | tf_op jit(solution)/shard_map/ppermute | solution.py:359
  7.9 1.3 %collective-permute-start.2 = (bf16[1040,128]{1,0:T(8,128)(2,1)S(1)}, bf16[1040,128]{1,0:T(8,128)(2,1)S(1)}, u32[]{:S(2)}, u32[]{:S(2)}) collective-permute-start(bf16[1040,128]{1,0:T(8,128)(2,1)S(1)} %get-tuple-element.31), channel_id=1, source_target_pairs={{0,4},{4,0},{8,12},{12,8},{1,5},{5,1},{9,13},{13,9},{2,6},{6,2},{1... | collective-permute-start | bytes 798728 | tf_op jit(solution)/shard_map/ppermute | solution.py:359
  9.2 0.0 copy-start.4
  9.2 1.6 %copy-done.4 = bf16[1,4,512,512]{3,2,1,0:T(8,128)(2,1)S(1)} copy-done((bf16[1,4,512,512]{3,2,1,0:T(8,128)(2,1)S(1)}, bf16[1,4,512,512]{3,2,1,0:T(8,128)(2,1)}, u32[]{:S(2)}) %copy-start.4) | copy-done | bytes 2097176
  10.8 0.0 copy-start.6
  10.8 0.9 %copy-done.6 = bf16[1,128,512]{2,1,0:T(8,128)(2,1)S(1)} copy-done((bf16[1,128,512]{2,1,0:T(8,128)(2,1)S(1)}, bf16[1,128,512]{2,1,0:T(8,128)(2,1)}, u32[]{:S(2)}) %copy-start.6) | copy-done | bytes 131096
  11.7 0.0 copy-start.7
  11.7 0.9 %copy-done.7 = bf16[1,512,128]{2,1,0:T(8,128)(2,1)S(1)} copy-done((bf16[1,512,128]{2,1,0:T(8,128)(2,1)S(1)}, bf16[1,512,128]{2,1,0:T(8,128)(2,1)}, u32[]{:S(2)}) %copy-start.7) | copy-done | bytes 131096
  12.6 0.0 copy-start.9
  12.6 0.7 %copy-done.9 = bf16[1,512]{1,0:T(2,128)(2,1)S(1)} copy-done((bf16[1,512]{1,0:T(2,128)(2,1)S(1)}, bf16[1,512]{1,0:T(2,128)(2,1)}, u32[]{:S(2)}) %copy-start.9) | copy-done | bytes 1048
  13.3 0.0 copy-start.5
  13.3 4.3 %mlp.4 = (bf16[1024,128]{1,0:T(8,128)(2,1)S(1)}, f32[8,256]{1,0:T(8,128)S(1)}) custom-call(bf16[1040,128]{1,0:T(8,128)(2,1)S(1)} %get-tuple-element.29.refs_0_.refs_8_, bf16[128,512]{1,0:T(8,128)(2,1)S(1)} %bitcast.17, bf16[4,512,512]{2,1,0:T(8,128)(2,1)S(1)} %bitcast.13, bf16[512,128]{1,0:T(8,128)(2,1)S(1)} %bitcast.21, bf16[1,512]{1,0:T(2,128)(2,1)S(1)} %copy-done.9), custom_call_target="tpu_custom_call" | custom-call | flops 2415919104 | tf_op jit(solution)/shard_map/mlp/pallas_call | solution.py:378
  17.6 2.2 %collective-permute-done.refs_0_.refs_10_ = bf16[1040,128]{1,0:T(8,128)(2,1)S(1)} collective-permute-done((bf16[1040,128]{1,0:T(8,128)(2,1)S(1)}, bf16[1040,128]{1,0:T(8,128)(2,1)S(1)}, u32[]{:S(2)}, u32[]{:S(2)}) %collective-permute-start) | collective-permute-done | bytes 266272 | tf_op jit(solution)/shard_map/ppermute | solution.py:359
  19.8 0.0 copy-start.8
  19.8 4.0 %collective-permute-start.1 = (bf16[1040,128]{1,0:T(8,128)(2,1)S(1)}, bf16[1040,128]{1,0:T(8,128)(2,1)S(1)}, u32[]{:S(2)}, u32[]{:S(2)}) collective-permute-start(bf16[1040,128]{1,0:T(8,128)(2,1)S(1)} %get-tuple-element.28), channel_id=1, source_target_pairs={{0,12},{4,8},{8,4},{12,0},{1,13},{5,9},{9,5},{13,1},{2,14},{6,10},... | collective-permute-start | bytes 798728 | tf_op jit(solution)/shard_map/ppermute | solution.py:359
  23.8 0.0 copy-done.5
  23.8 4.1 %mlp.6 = (bf16[1024,128]{1,0:T(8,128)(2,1)S(1)}, f32[8,256]{1,0:T(8,128)S(1)}) custom-call(bf16[1040,128]{1,0:T(8,128)(2,1)S(1)} %collective-permute-done.refs_0_.refs_10_, bf16[128,512]{1,0:T(8,128)(2,1)S(1)} %bitcast.18, bf16[4,512,512]{2,1,0:T(8,128)(2,1)S(1)} %bitcast.14, bf16[512,128]{1,0:T(8,128)(2,1)S(1)} %bitcast.22, bf16[1,512]{1,0:T(2,128)(2,1)S(1)} %copy-done.9), custom_call_target="tpu_custom_call" | custom-call | flops 2415919104 | tf_op jit(solution)/shard_map/mlp/pallas_call | solution.py:378
  27.8 0.0 copy-start.10
  27.9 0.0 collective-permute-done.2.refs_0_.refs_9_
  27.9 0.0 copy-done.8
  27.9 4.3 %mlp.5 = (bf16[1024,128]{1,0:T(8,128)(2,1)S(1)}, f32[8,256]{1,0:T(8,128)S(1)}) custom-call(bf16[1040,128]{1,0:T(8,128)(2,1)S(1)} %collective-permute-done.2.refs_0_.refs_9_, bf16[128,512]{1,0:T(8,128)(2,1)S(1)} %bitcast.19, bf16[4,512,512]{2,1,0:T(8,128)(2,1)S(1)} %bitcast.15, bf16[512,128]{1,0:T(8,128)(2,1)S(1)} %bitcast.23, bf16[1,512]{1,0:T(2,128)(2,1)S(1)} %copy-done.9), custom_call_target="tpu_custom_call" | custom-call | flops 2415919104 | tf_op jit(solution)/shard_map/mlp/pallas_call | solution.py:378
  32.1 0.0 collective-permute-done.1.refs_0_.refs_11_
  32.1 0.0 copy-done.10
  32.2 4.1 %mlp.7 = (bf16[1024,128]{1,0:T(8,128)(2,1)S(1)}, bf16[32,256]{1,0:T(8,128)(2,1)S(1)}) custom-call(bf16[1040,128]{1,0:T(8,128)(2,1)S(1)} %collective-permute-done.1.refs_0_.refs_11_, bf16[128,512]{1,0:T(8,128)(2,1)S(1)} %bitcast.20, bf16[4,512,512]{2,1,0:T(8,128)(2,1)S(1)} %bitcast.16, bf16[512,128]{1,0:T(8,128)(2,1)S(1)} %bitcast.24, ...), custom_call_target="tpu_custom_call" | custom-call | flops 2415919104 | tf_op jit(solution)/shard_map/mlp/pallas_call | solution.py:378
  36.2 0.0 copy-start
  36.3 1.0 %collective-permute-start.5 = (bf16[32,256]{1,0:T(8,128)(2,1)S(1)}, bf16[32,256]{1,0:T(8,128)(2,1)S(1)}, u32[]{:S(2)}, u32[]{:S(2)}) collective-permute-start(bf16[32,256]{1,0:T(8,128)(2,1)S(1)} %get-tuple-element.35.refs_0_), channel_id=1, source_target_pairs={{0,12},{4,8},{8,4},{12,0},{1,13},{5,9},{9,5},{13,1},{2,14},{6,10},... | collective-permute-start | bytes 49160 | tf_op jit(solution)/shard_map/ppermute | solution.py:359
  37.2 2.2 %collective-permute-start.4 = (bf16[32,256]{1,0:T(8,128)(2,1)S(1)}, bf16[32,256]{1,0:T(8,128)(2,1)S(1)}, u32[]{:S(2)}, u32[]{:S(2)}) collective-permute-start(bf16[32,256]{1,0:T(8,128)(2,1)S(1)} %get-tuple-element.35.refs_0_), channel_id=1, source_target_pairs={{0,8},{4,12},{8,0},{12,4},{1,9},{5,13},{9,1},{13,5},{2,10},{6,14},... | collective-permute-start | bytes 49160 | tf_op jit(solution)/shard_map/ppermute | solution.py:359
  39.5 0.4 collective-permute-start.3
  39.9 0.9 %collective-permute-done.5.refs_3_ = bf16[32,256]{1,0:T(8,128)(2,1)S(1)} collective-permute-done((bf16[32,256]{1,0:T(8,128)(2,1)S(1)}, bf16[32,256]{1,0:T(8,128)(2,1)S(1)}, u32[]{:S(2)}, u32[]{:S(2)}) %collective-permute-start.5) | collective-permute-done | bytes 16416 | tf_op jit(solution)/shard_map/ppermute | solution.py:359
  40.8 0.1 collective-permute-done.4.refs_2_
  40.9 1.5 %collective-permute-done.3.refs_1_ = bf16[32,256]{1,0:T(8,128)(2,1)S(1)} collective-permute-done((bf16[32,256]{1,0:T(8,128)(2,1)S(1)}, bf16[32,256]{1,0:T(8,128)(2,1)S(1)}, u32[]{:S(2)}, u32[]{:S(2)}) %collective-permute-start.3) | collective-permute-done | bytes 16416 | tf_op jit(solution)/shard_map/ppermute | solution.py:359
  42.4 2.0 %color.1 = (bf16[352,128]{1,0:T(8,128)(2,1)S(1)}, bf16[352,128]{1,0:T(8,128)(2,1)S(1)}, bf16[352,128]{1,0:T(8,128)(2,1)S(1)}, bf16[352,128]{1,0:T(8,128)(2,1)S(1)}) custom-call(s32[1]{0:T(128)} %bitcast.2.me_ref, bf16[32,256]{1,0:T(8,128)(2,1)S(1)} %get-tuple-element.35.refs_0_, bf16[32,256]{1,0:T(8,128)(2,1)S(1)} %collective-permute-done.3.refs_1_, ...), custom_call_target="tpu_custom_call" | custom-call | tf_op jit(solution)/shard_map/color/pallas_call | solution.py:398
  44.4 0.1 collective-permute-start.6
  44.5 1.4 %collective-permute-start.7 = (bf16[352,128]{1,0:T(8,128)(2,1)S(1)}, bf16[352,128]{1,0:T(8,128)(2,1)S(1)}, u32[]{:S(2)}, u32[]{:S(2)}) collective-permute-start(bf16[352,128]{1,0:T(8,128)(2,1)S(1)} %get-tuple-element.42), channel_id=1, source_target_pairs={{0,8},{4,12},{8,0},{12,4},{1,9},{5,13},{9,1},{13,5},{2,10},{6,14},... | collective-permute-start | bytes 270344 | tf_op jit(solution)/shard_map/ppermute | solution.py:359
  45.9 2.1 %collective-permute-start.8 = (bf16[352,128]{1,0:T(8,128)(2,1)S(1)}, bf16[352,128]{1,0:T(8,128)(2,1)S(1)}, u32[]{:S(2)}, u32[]{:S(2)}) collective-permute-start(bf16[352,128]{1,0:T(8,128)(2,1)S(1)} %get-tuple-element.43), channel_id=1, source_target_pairs={{0,12},{4,8},{8,4},{12,0},{1,13},{5,9},{9,5},{13,1},{2,14},{6,10},... | collective-permute-start | bytes 270344 | tf_op jit(solution)/shard_map/ppermute | solution.py:359
  48.0 0.0 collective-permute-done.6.refs_1_
  48.0 0.8 %collective-permute-done.7.refs_2_ = bf16[352,128]{1,0:T(8,128)(2,1)S(1)} collective-permute-done((bf16[352,128]{1,0:T(8,128)(2,1)S(1)}, bf16[352,128]{1,0:T(8,128)(2,1)S(1)}, u32[]{:S(2)}, u32[]{:S(2)}) %collective-permute-start.7) | collective-permute-done | bytes 90144 | tf_op jit(solution)/shard_map/ppermute | solution.py:359
  48.8 2.9 %collective-permute-done.8.refs_3_ = bf16[352,128]{1,0:T(8,128)(2,1)S(1)} collective-permute-done((bf16[352,128]{1,0:T(8,128)(2,1)S(1)}, bf16[352,128]{1,0:T(8,128)(2,1)S(1)}, u32[]{:S(2)}, u32[]{:S(2)}) %collective-permute-start.8) | collective-permute-done | bytes 90144 | tf_op jit(solution)/shard_map/ppermute | solution.py:359
  51.8 6.6 %collective-permute-start.9 = (bf16[80,128]{1,0:T(8,128)(2,1)S(1)}, bf16[80,128]{1,0:T(8,128)(2,1)S(1)}, u32[]{:S(2)}, u32[]{:S(2)}) collective-permute-start(bf16[80,128]{1,0:T(8,128)(2,1)S(1)} %get-tuple-element.45), channel_id=1, source_target_pairs={{0,1},{1,2},{2,3},{4,5},{5,6},{6,7},{8,9},{9,10},{10,11},{12,13},{... | collective-permute-start | bytes 61448 | tf_op jit(solution)/shard_map/ppermute | solution.py:424
  58.4 1.9 %collective-permute-start.10 = (bf16[80,128]{1,0:T(8,128)(2,1)S(1)}, bf16[80,128]{1,0:T(8,128)(2,1)S(1)}, u32[]{:S(2)}, u32[]{:S(2)}) collective-permute-start(bf16[80,128]{1,0:T(8,128)(2,1)S(1)} %get-tuple-element.46), channel_id=1, source_target_pairs={{1,0},{2,1},{3,2},{5,4},{6,5},{7,6},{9,8},{10,9},{11,10},{13,12},{... | collective-permute-start | bytes 61448 | tf_op jit(solution)/shard_map/ppermute | solution.py:425
  60.3 0.1 pad_add_fusion.place_ref
  60.4 0.0 collective-permute-done.9.above_ref
  60.4 3.1 %collective-permute-done.10.below_ref = bf16[80,128]{1,0:T(8,128)(2,1)S(1)} collective-permute-done((bf16[80,128]{1,0:T(8,128)(2,1)S(1)}, bf16[80,128]{1,0:T(8,128)(2,1)S(1)}, u32[]{:S(2)}, u32[]{:S(2)}) %collective-permute-start.10) | collective-permute-done | bytes 20512 | tf_op jit(solution)/shard_map/ppermute | solution.py:425
  63.5 0.0 copy-done
  63.5 2.9 %decode.1 = bf16[256,128]{1,0:T(8,128)(2,1)} custom-call(s32[4]{0:T(128)S(1)} %pad_add_fusion.place_ref, bf16[352,128]{1,0:T(8,128)(2,1)S(1)} %get-tuple-element.44.tile_ref, bf16[80,128]{1,0:T(8,128)(2,1)S(1)} %collective-permute-done.9.above_ref, bf16[80,128]{1,0:T(8,128)(2,1)S(1)} %collective-permute-done.10.below_ref, ...), custom_call_target="tpu_custom_call" | custom-call | tf_op jit(solution)/shard_map/decode/pallas_call | solution.py:430
  (2 shorter events, 0.1 us)
Async XLA Ops:
  0.0 1.0 %copy-start.1 = (bf16[1,1,2048,128]{3,2,1,0:T(8,128)(2,1)S(1)}, bf16[1,1,2048,128]{3,2,1,0:T(8,128)(2,1)}, u32[]{:S(2)}) copy-start(bf16[1,1,2048,128]{3,2,1,0:T(8,128)(2,1)} %param.8) | copy-start | bytes 1572868
  1.0 0.7 %copy-start.2 = (s32[1,1,2048,1]{2,3,1,0:T(1,128)S(1)}, s32[1,1,2048,1]{2,3,1,0:T(1,128)}, u32[]{:S(2)}) copy-start(s32[1,1,2048,1]{2,3,1,0:T(1,128)} %param.9) | copy-start | bytes 24580
  1.7 0.7 %copy-start.3 = (s32[1,1,8,256]{3,2,1,0:T(8,128)S(1)}, s32[1,1,8,256]{3,2,1,0:T(8,128)}, u32[]{:S(2)}) copy-start(s32[1,1,8,256]{3,2,1,0:T(8,128)} %param.10) | copy-start | bytes 24580
  4.8 15.0 %collective-permute-start = (bf16[1040,128]{1,0:T(8,128)(2,1)S(1)}, bf16[1040,128]{1,0:T(8,128)(2,1)S(1)}, u32[]{:S(2)}, u32[]{:S(2)}) collective-permute-start(bf16[1040,128]{1,0:T(8,128)(2,1)S(1)} %get-tuple-element.27), channel_id=1, source_target_pairs={{0,8},{4,12},{8,0},{12,4},{1,9},{5,13},{9,1},{13,5},{2,10},{6,14},... | collective-permute-start | bytes 798728 | tf_op jit(solution)/shard_map/ppermute | solution.py:359
  7.9 19.9 %collective-permute-start.2 = (bf16[1040,128]{1,0:T(8,128)(2,1)S(1)}, bf16[1040,128]{1,0:T(8,128)(2,1)S(1)}, u32[]{:S(2)}, u32[]{:S(2)}) collective-permute-start(bf16[1040,128]{1,0:T(8,128)(2,1)S(1)} %get-tuple-element.31), channel_id=1, source_target_pairs={{0,4},{4,0},{8,12},{12,8},{1,5},{5,1},{9,13},{13,9},{2,6},{6,2},{1... | collective-permute-start | bytes 798728 | tf_op jit(solution)/shard_map/ppermute | solution.py:359
  9.2 1.6 %copy-start.4 = (bf16[1,4,512,512]{3,2,1,0:T(8,128)(2,1)S(1)}, bf16[1,4,512,512]{3,2,1,0:T(8,128)(2,1)}, u32[]{:S(2)}) copy-start(bf16[1,4,512,512]{3,2,1,0:T(8,128)(2,1)} %param.12) | copy-start | bytes 6291460
  10.8 0.9 %copy-start.6 = (bf16[1,128,512]{2,1,0:T(8,128)(2,1)S(1)}, bf16[1,128,512]{2,1,0:T(8,128)(2,1)}, u32[]{:S(2)}) copy-start(bf16[1,128,512]{2,1,0:T(8,128)(2,1)} %param.11) | copy-start | bytes 393220
  11.7 0.9 %copy-start.7 = (bf16[1,512,128]{2,1,0:T(8,128)(2,1)S(1)}, bf16[1,512,128]{2,1,0:T(8,128)(2,1)}, u32[]{:S(2)}) copy-start(bf16[1,512,128]{2,1,0:T(8,128)(2,1)} %param.13) | copy-start | bytes 393220
  12.6 0.7 %copy-start.9 = (bf16[1,512]{1,0:T(2,128)(2,1)S(1)}, bf16[1,512]{1,0:T(2,128)(2,1)}, u32[]{:S(2)}) copy-start(bf16[1,512]{1,0:T(2,128)(2,1)} %refs_4_.7) | copy-start | bytes 3076
  13.3 10.4 %copy-start.5 = (bf16[1,4,512,512]{3,2,1,0:T(8,128)(2,1)S(1)}, bf16[1,4,512,512]{3,2,1,0:T(8,128)(2,1)}, u32[]{:S(2)}) copy-start(bf16[1,4,512,512]{3,2,1,0:T(8,128)(2,1)} %param.12) | copy-start | bytes 6291460
  19.8 8.1 %copy-start.8 = (bf16[1,512,128]{2,1,0:T(8,128)(2,1)S(1)}, bf16[1,512,128]{2,1,0:T(8,128)(2,1)}, u32[]{:S(2)}) copy-start(bf16[1,512,128]{2,1,0:T(8,128)(2,1)} %param.13) | copy-start | bytes 393220
  19.8 12.4 %collective-permute-start.1 = (bf16[1040,128]{1,0:T(8,128)(2,1)S(1)}, bf16[1040,128]{1,0:T(8,128)(2,1)S(1)}, u32[]{:S(2)}, u32[]{:S(2)}) collective-permute-start(bf16[1040,128]{1,0:T(8,128)(2,1)S(1)} %get-tuple-element.28), channel_id=1, source_target_pairs={{0,12},{4,8},{8,4},{12,0},{1,13},{5,9},{9,5},{13,1},{2,14},{6,10},... | collective-permute-start | bytes 798728 | tf_op jit(solution)/shard_map/ppermute | solution.py:359
  27.8 4.3 %copy-start.10 = (bf16[1,512]{1,0:T(2,128)(2,1)S(1)}, bf16[1,512]{1,0:T(2,128)(2,1)}, u32[]{:S(2)}) copy-start(bf16[1,512]{1,0:T(2,128)(2,1)} %refs_4_.7) | copy-start | bytes 3076
  36.2 27.2 %copy-start = (bf16[3,3,3,128,128]{4,3,2,1,0:T(8,128)(2,1)S(1)}, bf16[3,3,3,128,128]{4,3,2,1,0:T(8,128)(2,1)}, u32[]{:S(2)}) copy-start(bf16[3,3,3,128,128]{4,3,2,1,0:T(8,128)(2,1)} %w_ref.1) | copy-start | bytes 2654212
  36.3 4.6 %collective-permute-start.5 = (bf16[32,256]{1,0:T(8,128)(2,1)S(1)}, bf16[32,256]{1,0:T(8,128)(2,1)S(1)}, u32[]{:S(2)}, u32[]{:S(2)}) collective-permute-start(bf16[32,256]{1,0:T(8,128)(2,1)S(1)} %get-tuple-element.35.refs_0_), channel_id=1, source_target_pairs={{0,12},{4,8},{8,4},{12,0},{1,13},{5,9},{9,5},{13,1},{2,14},{6,10},... | collective-permute-start | bytes 49160 | tf_op jit(solution)/shard_map/ppermute | solution.py:359
  37.2 3.7 %collective-permute-start.4 = (bf16[32,256]{1,0:T(8,128)(2,1)S(1)}, bf16[32,256]{1,0:T(8,128)(2,1)S(1)}, u32[]{:S(2)}, u32[]{:S(2)}) collective-permute-start(bf16[32,256]{1,0:T(8,128)(2,1)S(1)} %get-tuple-element.35.refs_0_), channel_id=1, source_target_pairs={{0,8},{4,12},{8,0},{12,4},{1,9},{5,13},{9,1},{13,5},{2,10},{6,14},... | collective-permute-start | bytes 49160 | tf_op jit(solution)/shard_map/ppermute | solution.py:359
  39.5 2.9 %collective-permute-start.3 = (bf16[32,256]{1,0:T(8,128)(2,1)S(1)}, bf16[32,256]{1,0:T(8,128)(2,1)S(1)}, u32[]{:S(2)}, u32[]{:S(2)}) collective-permute-start(bf16[32,256]{1,0:T(8,128)(2,1)S(1)} %get-tuple-element.35.refs_0_), channel_id=1, source_target_pairs={{0,4},{4,0},{8,12},{12,8},{1,5},{5,1},{9,13},{13,9},{2,6},{6,2},{1... | collective-permute-start | bytes 49160 | tf_op jit(solution)/shard_map/ppermute | solution.py:359
  44.4 3.6 %collective-permute-start.6 = (bf16[352,128]{1,0:T(8,128)(2,1)S(1)}, bf16[352,128]{1,0:T(8,128)(2,1)S(1)}, u32[]{:S(2)}, u32[]{:S(2)}) collective-permute-start(bf16[352,128]{1,0:T(8,128)(2,1)S(1)} %get-tuple-element.41), channel_id=1, source_target_pairs={{0,4},{4,0},{8,12},{12,8},{1,5},{5,1},{9,13},{13,9},{2,6},{6,2},{1... | collective-permute-start | bytes 270344 | tf_op jit(solution)/shard_map/ppermute | solution.py:359
  44.5 4.3 %collective-permute-start.7 = (bf16[352,128]{1,0:T(8,128)(2,1)S(1)}, bf16[352,128]{1,0:T(8,128)(2,1)S(1)}, u32[]{:S(2)}, u32[]{:S(2)}) collective-permute-start(bf16[352,128]{1,0:T(8,128)(2,1)S(1)} %get-tuple-element.42), channel_id=1, source_target_pairs={{0,8},{4,12},{8,0},{12,4},{1,9},{5,13},{9,1},{13,5},{2,10},{6,14},... | collective-permute-start | bytes 270344 | tf_op jit(solution)/shard_map/ppermute | solution.py:359
  45.9 5.9 %collective-permute-start.8 = (bf16[352,128]{1,0:T(8,128)(2,1)S(1)}, bf16[352,128]{1,0:T(8,128)(2,1)S(1)}, u32[]{:S(2)}, u32[]{:S(2)}) collective-permute-start(bf16[352,128]{1,0:T(8,128)(2,1)S(1)} %get-tuple-element.43), channel_id=1, source_target_pairs={{0,12},{4,8},{8,4},{12,0},{1,13},{5,9},{9,5},{13,1},{2,14},{6,10},... | collective-permute-start | bytes 270344 | tf_op jit(solution)/shard_map/ppermute | solution.py:359
  51.8 8.6 %collective-permute-start.9 = (bf16[80,128]{1,0:T(8,128)(2,1)S(1)}, bf16[80,128]{1,0:T(8,128)(2,1)S(1)}, u32[]{:S(2)}, u32[]{:S(2)}) collective-permute-start(bf16[80,128]{1,0:T(8,128)(2,1)S(1)} %get-tuple-element.45), channel_id=1, source_target_pairs={{0,1},{1,2},{2,3},{4,5},{5,6},{6,7},{8,9},{9,10},{10,11},{12,13},{... | collective-permute-start | bytes 61448 | tf_op jit(solution)/shard_map/ppermute | solution.py:424
  58.4 5.1 %collective-permute-start.10 = (bf16[80,128]{1,0:T(8,128)(2,1)S(1)}, bf16[80,128]{1,0:T(8,128)(2,1)S(1)}, u32[]{:S(2)}, u32[]{:S(2)}) collective-permute-start(bf16[80,128]{1,0:T(8,128)(2,1)S(1)} %get-tuple-element.46), channel_id=1, source_target_pairs={{1,0},{2,1},{3,2},{5,4},{6,5},{7,6},{9,8},{10,9},{11,10},{13,12},{... | collective-permute-start | bytes 61448 | tf_op jit(solution)/shard_map/ppermute | solution.py:425
